TPU v7x, 32 devices: a whole 2x2x4 slice. The times are simulated.
32 devices in a mesh: band: 4 (over y, x), row: 8 (over z, core).
Axes of the slice: x: 2, y: 2, z: 4, core: 2. Of those that a mesh axis runs over, the one named last changes fastest.
Arguments:
- amplitude: bfloat16 [512, 8192], P('row'), may hold values from 0.5 to 1.5
- seg_map: int32 [512, 8192], P('row'), may hold values from 0 to 1199, as said below
- seg_box: int32 [4, 1200], replicated, may hold values from 0 to 8191, as said below
- seg_coeffs: float32 [3, 1200], replicated, may hold values from -1 to 1
- probe_freq: int32 [2, 2], replicated, may hold values from 3 to 23
- probe_amp: float32 [2], replicated, may hold values from 0.3 to 0.8
- measured: float32 [8, 256, 4, 2, 256], P('band', 'row'), may hold values from -6 to 6
Outputs:
- gradient: float32 [3, 1200], replicated
Inputs may be any that keep to these rules, and one draw needn't show every extreme that they name: `seg_map`: segments lie in 16 rows of rectangular tiles of whole pupil rows, 75 tiles side by side in each, alternate rows offset by half a tile; segment numbers rise by tile row, then by column; every segment has samples. `seg_box`: the bounds of each segment's samples in seg_map, rows first.
All inputs are finite; a program needn't handle non-finite values.
Results may differ from a plain program's by a relative error of at most 0.0015.
Values may be sent and summed in bfloat16 or wider, within the bound.
No kernel may reach another device: no remote copies, remote signals or barrier semaphores. Data moves between devices by JAX's collectives and lax.ppermute only.
A program may use at most 192 MiB of HBM per device.

v0:
```python
import functools
import math

import jax
import jax.numpy as jnp
from jax import lax
from jax.experimental import pallas as pl
from jax.experimental.pallas import tpu as pltpu
from jax.sharding import PartitionSpec as P

SROWS = 16
SAMPLING = 0.5
SPREAD = 0.2
TWO_PI = 2.0 * math.pi
LANES = 128
F32 = jnp.float32
BF16 = jnp.bfloat16

SIN_HALF = (0.9999999971, -0.1666666029, 0.008333109246, -0.0001981365728, 2.616271295e-06)
COS_HALF = (0.9999999682, -0.4999993032, 0.04166421727, -0.001385868782, 2.327410856e-05)
SIN_WAVE = (0.9999999964, -0.166666488, 0.008331936401, -0.000194912576)
COS_WAVE = (0.9999999679, -0.499998396, 0.04165412354, -0.001357443708)
SIN_TURN = (
    6.283185307, -41.34170222, 81.60524741, -76.70580003,
    42.05775188, -15.08655272, 3.781282403, -0.6207370354,
)
COS_TURN = (
    0.9999999999, -19.73920874, 64.93938905, -85.45665775,
    60.24212493, -26.40463062, 7.800022219, -1.452987552,
)


def series(coeffs, t):
    value = jnp.full_like(t, coeffs[-1])
    for c in reversed(coeffs[:-1]):
        value = value * t + c
    return value


def turn_cos_sin(turns):
    t = turns - jnp.floor(turns + 0.5)
    square = t * t
    return series(COS_TURN, square), t * series(SIN_TURN, square)


def iota(shape, axis):
    return lax.broadcasted_iota(jnp.int32, shape, axis)


def focal_scale(m_positive, band, band_total):
    ratio = 1.0 + SPREAD * ((band.astype(F32) + 0.5) / band_total - 0.5)
    return m_positive / ratio


def band_lanes(first_band, bands, half, band_total, rows):
    pieces = []
    for b in range(bands):
        q = (iota((rows, half), 1).astype(F32) + 0.5) * SAMPLING
        band = jnp.full((rows, half), 1, jnp.int32) * (first_band + b)
        pieces.append(focal_scale(q, band, band_total))
    return jnp.concatenate(pieces, axis=1)


def column_tables(first_band, bands, half, band_total, cols, tile_ref, shift_ref):
    q = band_lanes(first_band, bands, half, band_total, LANES)
    c, s = turn_cos_sin(q * (iota(q.shape, 0).astype(F32) / cols))
    tile_ref[0] = c
    tile_ref[1] = s
    tiles = cols // LANES
    q = band_lanes(first_band, bands, half, band_total, tiles)
    x = (iota(q.shape, 0).astype(F32) * LANES + 0.5) / cols - 0.5
    c, s = turn_cos_sin(q * x)
    shift_ref[0] = c
    shift_ref[1] = s


def write_table(table_ref, tile_ref, shift_ref, first_tile, tiles, bands, half):
    for i in range(tiles):
        sc = shift_ref[0, pl.ds(first_tile + i, 1), :]
        ss = shift_ref[1, pl.ds(first_tile + i, 1), :]
        for b in range(bands):
            lanes = slice(b * half, (b + 1) * half)
            for k in range(0, LANES, 16):
                tc = tile_ref[0, k : k + 16, lanes]
                ts = tile_ref[1, k : k + 16, lanes]
                rows = slice(i * LANES + k, i * LANES + k + 16)
                table_ref[rows, 2 * b * half : (2 * b + 1) * half] = (
                    tc * sc[:, lanes] - ts * ss[:, lanes]
                ).astype(BF16)
                table_ref[rows, (2 * b + 1) * half : (2 * b + 2) * half] = (
                    ts * sc[:, lanes] + tc * ss[:, lanes]
                ).astype(BF16)


def tile_row_pieces(seg_ref, per_row, width):
    for t in range(SROWS):
        yield t, pltpu.roll(seg_ref[...], (width - t * per_row) % width, axis=1)[:, :LANES]


def field_kernel(
    dims, pos_ref, box_ref, freq_ref, amp_ref, seg_ref, amplitude_ref, map_ref,
    x_ref, across_ref, y_ref,
    tables, bases, slot_tables, waves, tile_ref, shift_ref, table_ref, total_ref, slot_map,
):
    rows, cols, block, bands, half, band_total, total_rows, per_row, pairs, vloc, owners = dims
    step = pl.program_id(0)
    row0 = pos_ref[0] * rows

    @pl.when(step == 0)
    def _():
        width = seg_ref.shape[1]
        for g in range(rows // 8):
            here = (row0 + g * 8 + iota((8, LANES), 0)).astype(F32)
            values = [jnp.zeros((8, LANES), F32)] * 4
            base = jnp.zeros((8, LANES), jnp.int32)
            for t, piece in tile_row_pieces(seg_ref, per_row, width):
                part = [jnp.broadcast_to(piece[k : k + 1], (8, LANES)) for k in range(7)]
                low, high = part[3][:, :1], part[4][:, :1]
                mine = (here >= low) & (here <= high)
                down = (here - 0.5 * (part[3] + part[4])) / (0.5 * (part[4] - part[3] + 1.0))
                new = (
                    0.5 * (part[0] + part[2] * down),
                    0.5 * part[1],
                    0.5 * (part[5] + part[6]),
                    2.0 / (part[6] - part[5] + 1.0),
                )
                values = [jnp.where(mine, n, v) for n, v in zip(new, values)]
                base = jnp.where(mine, t * per_row, base)
            for k in range(4):
                tables[k, g * 8 : (g + 1) * 8] = values[k]
            bases[g * 8 : (g + 1) * 8] = base
        for t, piece in tile_row_pieces(seg_ref, per_row, width):
            slot_tables[0, t : t + 1] = 0.5 * (piece[5:6] + piece[6:7])
            slot_tables[1, t : t + 1] = 2.0 / (piece[6:7] - piece[5:6] + 1.0)
        y = ((row0 + iota((rows, LANES), 0)).astype(F32) + 0.5) / cols - total_rows / (2.0 * cols)
        for j in range(pairs):
            c, s = turn_cos_sin(freq_ref[j, 1].astype(F32) * y)
            waves[2 * j] = amp_ref[j] * c
            waves[2 * j + 1] = amp_ref[j] * s
        column_tables(pos_ref[1] * bands, bands, half, band_total, cols, tile_ref, shift_ref)
        total_ref[...] = jnp.zeros_like(total_ref)

    for t in range(SROWS):
        first = jnp.clip(box_ref[0, t * per_row] - row0, 0, rows - 1)
        slot_map[t : t + 1, :] = map_ref[pl.ds(first, 1), :] - t * per_row
    chunks = block // LANES
    for i in range(chunks):
        lanes = slice(i * LANES, (i + 1) * LANES)
        column = (iota((8, LANES), 1) + (step * block + i * LANES)).astype(F32)
        for t in range(0, SROWS, 8):
            index = slot_map[t : t + 8, lanes] & (LANES - 1)
            mid = jnp.take_along_axis(slot_tables[0, t : t + 8], index, axis=1)
            inv = jnp.take_along_axis(slot_tables[1, t : t + 8], index, axis=1)
            across_ref[t : t + 8, lanes] = (column - mid) * inv

    row = iota((8, block), 0)
    freq = jnp.zeros((8, block), F32)
    for j in range(pairs):
        freq = jnp.where(row // 2 == j, freq_ref[j, 0].astype(F32), freq)
    x = ((iota((8, block), 1) + step * block).astype(F32) + 0.5) / cols - 0.5
    turn_c, turn_s = turn_cos_sin(freq * x)
    columns_wave = jnp.where(row % 2 == 0, turn_s, turn_c)

    write_table(table_ref, tile_ref, shift_ref, step * chunks, chunks, bands, half)

    for i in range(chunks):
        lanes = slice(i * LANES, (i + 1) * LANES)
        column = (iota((16, LANES), 1) + (step * block + i * LANES)).astype(F32)
        for g in range(0, rows, 16):
            here = slice(g, g + 16)
            index = map_ref[here, lanes] - bases[here]

            def pick(k):
                return jnp.concatenate(
                    [
                        jnp.take_along_axis(tables[k, g + h : g + h + 8], index[h : h + 8], axis=1)
                        for h in (0, 8)
                    ],
                    axis=0,
                )

            half_phase = pick(0) + pick(1) * ((column - pick(2)) * pick(3))
            square = half_phase * half_phase
            s = half_phase * series(SIN_HALF, square)
            c = series(COS_HALF, square)
            twice = s + s
            size = amplitude_ref[here, lanes].astype(F32)
            real = size * (1.0 - twice * s)
            imag = size * (twice * c)
            for j in range(pairs):
                wave = (
                    columns_wave[2 * j : 2 * j + 1, lanes] * waves[2 * j, here]
                    + columns_wave[2 * j + 1 : 2 * j + 2, lanes] * waves[2 * j + 1, here]
                )
                square = wave * wave
                parts = (series(COS_WAVE, square), wave * series(SIN_WAVE, square))
                for k in range(2):
                    at = (2 * j + k) * 2 * rows + g
                    x_ref[at : at + 16, lanes] = (real * parts[k]).astype(BF16)
                    x_ref[at + rows : at + rows + 16, lanes] = (imag * parts[k]).astype(BF16)

    total_ref[...] += jnp.dot(x_ref[...], table_ref[...], preferred_element_type=F32)

    @pl.when(step == pl.num_programs(0) - 1)
    def _():
        r2 = 2 * rows
        m = iota((half, half), 0)
        n = iota((half, half), 1)
        straight = (m == n).astype(F32).astype(BF16)
        turned = (m + n == half - 1).astype(F32).astype(BF16)
        for b in range(bands):
            for p in range(2 * pairs):
                cos_part = total_ref[p * r2 : (p + 1) * r2, 2 * b * half : (2 * b + 1) * half]
                sin_part = total_ref[p * r2 : (p + 1) * r2, (2 * b + 1) * half : (2 * b + 2) * half]
                swapped = jnp.concatenate([sin_part[rows:], -sin_part[:rows]], axis=0)
                nt = (((1,), (1,)), ((), ()))
                low = lax.dot_general(
                    turned, (cos_part - swapped).astype(BF16), nt, preferred_element_type=F32
                ).astype(BF16)
                high = lax.dot_general(
                    straight, (cos_part + swapped).astype(BF16), nt, preferred_element_type=F32
                ).astype(BF16)
                if owners:
                    each = half // vloc
                    for d in range(each):
                        piece = slice(d * vloc, (d + 1) * vloc)
                        y_ref[d, b, p * vloc : (p + 1) * vloc, :] = low[piece]
                        y_ref[each + d, b, p * vloc : (p + 1) * vloc, :] = high[piece]
                else:
                    y_ref[b, p, :half, :] = low
                    y_ref[b, p, half:, :] = high


def focal_kernel(dims, pos_ref, y_ref, measured_ref, h_ref, table_ref):
    rows, cols, bands, focal, band_total, total_rows, sources, scale = dims
    r2 = 2 * rows
    for b in range(bands):
        band = jnp.full((rows, focal), 1, jnp.int32) * (pos_ref[1] * bands + b)
        q = (iota((rows, focal), 1).astype(F32) + (0.5 - focal / 2)) * SAMPLING
        q = focal_scale(q, band, band_total)
        tile_c, tile_s = turn_cos_sin(q * (iota(q.shape, 0).astype(F32) / cols))
        first = iota((sources, focal), 0).astype(F32) * rows + 0.5
        y = first / cols - total_rows / (2.0 * cols)
        shift_c, shift_s = turn_cos_sin(jnp.broadcast_to(q[:1], y.shape) * y)
        for d in range(sources):
            sc, ss = shift_c[d : d + 1], shift_s[d : d + 1]
            c = (tile_c * sc - tile_s * ss).astype(BF16)
            s_value = tile_s * sc + tile_c * ss
            s = s_value.astype(BF16)
            table_ref[d * r2 : d * r2 + rows, :focal] = c
            table_ref[d * r2 : d * r2 + rows, focal:] = (-s_value).astype(BF16)
            table_ref[d * r2 + rows : (d + 1) * r2, :focal] = s
            table_ref[d * r2 + rows : (d + 1) * r2, focal:] = c
        lhs = jnp.concatenate([y_ref[d, b] for d in range(sources)], axis=1)
        f = jnp.dot(lhs, table_ref[...], preferred_element_type=F32)
        residual = (f * (2.0 * scale) - measured_ref[b]).astype(BF16)
        spread = lax.dot_general(
            residual, table_ref[...], (((1,), (1,)), ((), ())), preferred_element_type=F32
        )
        for d in range(sources):
            h_ref[d, b] = spread[:, d * r2 : (d + 1) * r2].astype(BF16)


def weight_kernel(
    dims, pos_ref, box_ref, seg_ref, h_ref, x_ref, across_ref, out_ref,
    left_ref, pick_ref, tile_ref, shift_ref, table_ref, g_ref, weight_ref, sums_ref, slot_ref,
):
    (
        rows, cols, block, bands, half, band_total, per_row, pairs, vloc, sources, scale
    ) = dims
    step = pl.program_id(0)
    row0 = pos_ref[0] * rows
    r2 = 2 * rows
    nt = (((1,), (1,)), ((), ()))

    @pl.when(step == 0)
    def _():
        column_tables(pos_ref[1] * bands, bands, half, band_total, cols, tile_ref, shift_ref)
        m = iota((half, 2 * half), 0)
        v = iota((half, 2 * half), 1)
        upper = (v == half + m).astype(F32)
        lower = (v == half - 1 - m).astype(F32)
        even, odd = (upper + lower).astype(BF16), (upper - lower).astype(BF16)
        same = (iota((r2, r2), 0) == iota((r2, r2), 1)).astype(F32).astype(BF16)
        for b in range(bands):
            for p in range(2 * pairs):
                if sources:
                    block_h = jnp.concatenate(
                        [h_ref[d, b, p * vloc : (p + 1) * vloc, :] for d in range(sources)], axis=0
                    )
                else:
                    block_h = h_ref[b, p]

                def fold(mirror):
                    folded = jnp.dot(mirror, block_h, preferred_element_type=F32).astype(BF16)
                    return lax.dot_general(same, folded, nt, preferred_element_type=F32)

                plus, minus = fold(even), fold(odd)
                at = slice(p * r2, (p + 1) * r2)
                left_ref[at, 2 * b * half : (2 * b + 1) * half] = plus.astype(BF16)
                left_ref[at, (2 * b + 1) * half : (2 * b + 2) * half] = jnp.concatenate(
                    [-minus[rows:], minus[:rows]], axis=0
                ).astype(BF16)
        slot = iota((SROWS, r2), 0)
        lane = iota((SROWS, r2), 1)
        here = (row0 + lane % rows).astype(F32)
        low = jnp.zeros((SROWS, r2), F32)
        high = jnp.zeros((SROWS, r2), F32)
        for t in range(SROWS):
            low = jnp.where(slot == t, box_ref[0, t * per_row].astype(F32), low)
            high = jnp.where(slot == t, box_ref[1, t * per_row].astype(F32), high)
        mine = ((here >= low) & (here <= high)).astype(F32)
        down = mine * ((here - 0.5 * (low + high)) / (0.5 * (high - low + 1.0)))
        down_high = down.astype(BF16)
        pick_ref[:SROWS] = mine.astype(BF16)
        pick_ref[SROWS : 2 * SROWS] = down_high
        pick_ref[2 * SROWS :] = (down - down_high.astype(F32)).astype(BF16)
        out_ref[...] = jnp.zeros_like(out_ref)

    chunks = block // LANES
    write_table(table_ref, tile_ref, shift_ref, step * chunks, chunks, bands, half)
    g_ref[...] = lax.dot_general(left_ref[...], table_ref[...], nt, preferred_element_type=F32)
    for i in range(chunks):
        lanes = slice(i * LANES, (i + 1) * LANES)
        for g in range(0, rows, 16):
            value = jnp.zeros((16, LANES), F32)
            for p in range(2 * pairs):
                re = slice(p * r2 + g, p * r2 + g + 16)
                im = slice(p * r2 + rows + g, p * r2 + rows + g + 16)
                value = value + (
                    x_ref[re, lanes].astype(F32) * g_ref[im, lanes]
                    - x_ref[im, lanes].astype(F32) * g_ref[re, lanes]
                )
            high = value.astype(BF16)
            weight_ref[g : g + 16, lanes] = high
            weight_ref[rows + g : rows + g + 16, lanes] = (value - high.astype(F32)).astype(BF16)
    sums = jnp.dot(pick_ref[...], weight_ref[...], preferred_element_type=F32)
    sums_ref[step, 0] = sums[:SROWS]
    sums_ref[step, 1] = sums[:SROWS] * across_ref[...]
    sums_ref[step, 2] = sums[SROWS : 2 * SROWS] + sums[2 * SROWS :]

    @pl.when(step == pl.num_programs(0) - 1)
    def _():
        width = seg_ref.shape[1]
        for t, piece in tile_row_pieces(seg_ref, per_row, width):
            top, bottom = box_ref[0, t * per_row], box_ref[1, t * per_row]

            @pl.when((top < row0 + rows) & (bottom >= row0))
            def _():
                left, right = piece[5:6], piece[6:7]
                slot_ref[...] = jnp.zeros_like(slot_ref)

                def add(i, carry):
                    column = (iota((block, LANES), 0) + i * block).astype(F32)
                    inside = ((column >= left) & (column <= right)).astype(F32).astype(BF16)
                    terms = [sums_ref[i, q, t : t + 1, :] for q in range(3)]
                    highs = [x.astype(BF16) for x in terms]
                    lows = [(x - h.astype(F32)) for x, h in zip(terms, highs)]
                    stacked = jnp.concatenate(
                        [h.astype(F32) for h in highs] + lows + lows[:2], axis=0
                    ).astype(BF16)
                    slot_ref[...] += jnp.dot(stacked, inside, preferred_element_type=F32)
                    return carry

                lax.fori_loop(0, pl.num_programs(0), add, 0)
                for q in range(3):
                    out_ref[q, t : t + 1] = (slot_ref[q : q + 1] + slot_ref[q + 3 : q + 4]) * scale


def body(amplitude, seg_map, seg_box, seg_coeffs, probe_freq, probe_amp, measured):
    rows, cols = amplitude.shape
    owners = lax.axis_size("row")
    band_axis = lax.axis_size("band")
    total_rows = rows * owners
    bands, vloc, probes, _, focal = measured.shape
    pairs = probes // 2
    half = focal // 2
    band_total = bands * band_axis
    segments = seg_coeffs.shape[1]
    per_row = segments // SROWS
    arrays = 2 * pairs
    r2 = 2 * rows
    normf = 1.0 / math.sqrt(total_rows * cols)
    aligned = vloc % 16 == 0
    block = 512
    steps = cols // block

    pos = jnp.stack([lax.axis_index("row"), lax.axis_index("band")]).astype(jnp.int32)
    width = -(-(segments + LANES) // LANES) * LANES
    seg_table = jnp.pad(
        jnp.concatenate([seg_coeffs, seg_box.astype(F32)], axis=0), ((0, 1), (0, width - segments))
    )
    smem = pl.BlockSpec(memory_space=pltpu.SMEM)
    whole = pl.BlockSpec(memory_space=pltpu.VMEM)
    k_width = 2 * bands * half

    def resident(shape):
        return pl.BlockSpec(shape, lambda i: (0,) * len(shape), pipeline_mode=pl.Buffered(1))

    y_shape = (owners, bands, arrays * vloc, r2) if aligned else (bands, arrays, focal, r2)
    fields, across, half_way = pl.pallas_call(
        functools.partial(
            field_kernel,
            (rows, cols, block, bands, half, band_total, total_rows, per_row, pairs, vloc, aligned),
        ),
        grid=(steps,),
        in_specs=[
            smem, smem, smem, smem,
            resident((8, width)),
            pl.BlockSpec((rows, block), lambda i: (0, i)),
            pl.BlockSpec((rows, block), lambda i: (0, i)),
        ],
        out_specs=[
            pl.BlockSpec((arrays * r2, block), lambda i: (0, i)),
            pl.BlockSpec((SROWS, block), lambda i: (0, i)),
            pl.BlockSpec(y_shape, lambda i: (0,) * len(y_shape)),
        ],
        out_shape=[
            jax.ShapeDtypeStruct((arrays * r2, cols), BF16),
            jax.ShapeDtypeStruct((SROWS, cols), F32),
            jax.ShapeDtypeStruct(y_shape, BF16),
        ],
        scratch_shapes=[
            pltpu.VMEM((4, rows, LANES), F32),
            pltpu.VMEM((rows, LANES), jnp.int32),
            pltpu.VMEM((2, SROWS, LANES), F32),
            pltpu.VMEM((2 * pairs, rows, LANES), F32),
            pltpu.VMEM((2, LANES, bands * half), F32),
            pltpu.VMEM((2, cols // LANES, bands * half), F32),
            pltpu.VMEM((block, k_width), BF16),
            pltpu.VMEM((arrays * r2, k_width), F32),
            pltpu.VMEM((SROWS, block), jnp.int32),
        ],
        compiler_params=pltpu.CompilerParams(dimension_semantics=("arbitrary",)),
        name="field",
    )(pos, seg_box, probe_freq, probe_amp, seg_table, amplitude, seg_map)

    if not aligned:
        half_way = (
            half_way.reshape(bands, arrays, owners, vloc, r2)
            .transpose(2, 0, 1, 3, 4)
            .reshape(owners, bands, arrays * vloc, r2)
        )
    regrouped = lax.all_to_all(half_way, "row", split_axis=0, concat_axis=0, tiled=True)

    plus, minus = measured[:, :, 0::2], measured[:, :, 1::2]
    total, difference = plus + minus, plus - minus
    turned = jnp.stack([difference[:, :, :, 1], -difference[:, :, :, 0]], axis=3)
    targets = jnp.stack([total, turned], axis=3)
    targets = targets.transpose(0, 2, 3, 1, 4, 5).reshape(bands, arrays * vloc, 2 * focal)

    spread = pl.pallas_call(
        functools.partial(
            focal_kernel, (rows, cols, bands, focal, band_total, total_rows, owners, normf)
        ),
        in_specs=[smem, whole, whole],
        out_specs=whole,
        out_shape=jax.ShapeDtypeStruct((owners, bands, arrays * vloc, r2), BF16),
        scratch_shapes=[pltpu.VMEM((owners * r2, 2 * focal), BF16)],
        name="focal",
    )(pos, regrouped, targets)

    hidden = lax.all_to_all(spread, "row", split_axis=0, concat_axis=0, tiled=True)
    if not aligned:
        hidden = (
            hidden.reshape(owners, bands, arrays, vloc, r2)
            .transpose(1, 2, 0, 3, 4)
            .reshape(bands, arrays, focal, r2)
        )

    scale = 2.0 * normf / (band_total * probes)
    local = pl.pallas_call(
        functools.partial(
            weight_kernel,
            (
                rows, cols, block, bands, half, band_total, per_row, pairs, vloc,
                owners if aligned else 0, scale,
            ),
        ),
        grid=(steps,),
        in_specs=[
            smem, smem,
            resident((8, width)),
            resident(hidden.shape),
            pl.BlockSpec((arrays * r2, block), lambda i: (0, i)),
            pl.BlockSpec((SROWS, block), lambda i: (0, i)),
        ],
        out_specs=pl.BlockSpec((3, SROWS, LANES), lambda i: (0, 0, 0)),
        out_shape=jax.ShapeDtypeStruct((3, SROWS, LANES), F32),
        scratch_shapes=[
            pltpu.VMEM((arrays * r2, k_width), BF16),
            pltpu.VMEM((3 * SROWS, r2), BF16),
            pltpu.VMEM((2, LANES, bands * half), F32),
            pltpu.VMEM((2, cols // LANES, bands * half), F32),
            pltpu.VMEM((block, k_width), BF16),
            pltpu.VMEM((arrays * r2, block), F32),
            pltpu.VMEM((r2, block), BF16),
            pltpu.VMEM((steps, 3, SROWS, block), F32),
            pltpu.VMEM((8, LANES), F32),
        ],
        compiler_params=pltpu.CompilerParams(dimension_semantics=("arbitrary",)),
        name="weight",
    )(pos, seg_box, seg_table, hidden, fields, across)

    devices = owners * band_axis
    axes = ("band", "row")
    shares = local.reshape(devices, -1)
    mine = jnp.sum(lax.all_to_all(shares, axes, split_axis=0, concat_axis=0, tiled=True), axis=0)
    copies = jnp.broadcast_to(mine[None], shares.shape)
    gathered = lax.all_to_all(copies, axes, split_axis=0, concat_axis=0, tiled=True)
    return gathered.reshape(3, SROWS, LANES)[:, :, :per_row].reshape(3, segments)


def solution(mesh):
    in_specs = (
        P("row", None),
        P("row", None),
        P(),
        P(),
        P(),
        P(),
        P("band", "row", None, None, None),
    )
    return jax.shard_map(body, mesh=mesh, in_specs=in_specs, out_specs=P(), check_vma=False)
```

profile of v0, /device:TPU:0, one launch (start us, length us, event | category | flops | bytes accessed | tf_op | source)
XLA Modules:
  0.0 118.8 jit_solution(5108148427402722860)
XLA Ops:
  0.0 0.7 convert_element_type.5
  0.7 0.6 pad_add_fusion.pos_ref
  1.3 1.4 %select_maximum_fusion.seg_ref = f32[8,1408]{1,0:T(8,128)} fusion(f32[4,1200]{1,0:T(4,128)S(1)} %convert_element_type.5, f32[3,1200]{1,0:T(4,128)} %param.10), kind=kLoop, calls=%fused_computation.5 | loop fusion | flops 90112 | bytes 78656 | tf_op jit(solution)/shard_map/concatenate | solution.py:391
  2.7 20.6 %field.1 = (bf16[512,8192]{1,0:T(8,128)(2,1)}, f32[16,8192]{1,0:T(8,128)}, bf16[8,2,128,128]{3,2,1,0:T(8,128)(2,1)}) custom-call(s32[2]{0:T(128)} %pad_add_fusion.pos_ref, s32[4,1200]{1,0:T(4,128)} %box_ref.3, s32[2,2]{1,0:T(2,128)} %freq_ref.1, f32[2]{0:T(128)} %amp_ref.1, f32[8,1408]{1,0:T(8,128)} %select_maximum_fusion.seg_ref, ...), custom_call_target="tpu_custom_call" | custom-call | tf_op jit(solution)/shard_map/field/pallas_call | solution.py:401
  23.3 6.4 %all-to-all-start = ((bf16[8,2,128,128]{3,2,1,0:T(8,128)(2,1)}), bf16[8,2,128,128]{3,2,1,0:T(8,128)(2,1)S(1)}, u32[]{:S(2)}, u32[]{:S(2)}) async-start(bf16[8,2,128,128]{3,2,1,0:T(8,128)(2,1)} %get-tuple-element.8), calls=%async_computation | async-start | bytes 1048576 | tf_op jit(solution)/shard_map/all_to_all | solution.py:444
  29.7 1.2 %add_bitcast_fusion = (f32[2,32,2,1,2,256]{5,4,2,1,0,3:T(2,128)S(1)}, f32[2,32,2,2,256]{4,3,2,1,0:T(2,128)S(1)}) fusion(f32[2,32,4,2,256]{4,3,2,1,0:T(2,128)} %param.13), kind=kLoop, calls=%fused_computation.2 | loop fusion | flops 131072 | bytes 1048576 | tf_op jit(solution)/shard_map/stack | solution.py:449
  30.9 0.2 fusion
  31.1 0.2 maximum_bitcast_fusion.1
  31.4 0.2 maximum_bitcast_fusion
  31.6 0.2 copy.9
  31.8 1.2 %reshape.20.measured_ref = f32[2,128,512]{2,1,0:T(8,128)} reshape(f32[2,2,2,32,2,256]{5,4,3,2,1,0:T(2,128)S(1)} %copy.9) | data formatting | bytes 1048576 | tf_op jit(solution)/shard_map/reshape | solution.py:450
  33.0 12.0 %all-to-all-done.y_ref = bf16[8,2,128,128]{3,2,1,0:T(8,128)(2,1)S(1)} async-done(((bf16[8,2,128,128]{3,2,1,0:T(8,128)(2,1)}), bf16[8,2,128,128]{3,2,1,0:T(8,128)(2,1)S(1)}, u32[]{:S(2)}, u32[]{:S(2)}) %all-to-all-start) | async-done | bytes 524320 | tf_op jit(solution)/shard_map/all_to_all | solution.py:444
  45.0 0.0 copy-start
  45.0 0.9 copy-done
  45.9 3.4 %focal.1 = bf16[8,2,128,128]{3,2,1,0:T(8,128)(2,1)} custom-call(s32[2]{0:T(128)} %pad_add_fusion.pos_ref, bf16[8,2,128,128]{3,2,1,0:T(8,128)(2,1)} %copy-done, f32[2,128,512]{2,1,0:T(8,128)} %reshape.20.measured_ref), custom_call_target="tpu_custom_call" | custom-call | tf_op jit(solution)/shard_map/focal/pallas_call | solution.py:452
  49.3 19.5 %all_to_all.26.h_ref = bf16[8,2,128,128]{3,2,1,0:T(8,128)(2,1)} all-to-all(bf16[8,2,128,128]{3,2,1,0:T(8,128)(2,1)} %focal.1), channel_id=1, replica_groups=mesh['band'=4,'row'=8] {'row'}, dimensions={0} | all-to-all | bytes 1048576 | tf_op jit(solution)/shard_map/all_to_all | solution.py:463
  68.8 24.2 %weight.1 = f32[3,16,128]{2,1,0:T(8,128)} custom-call(s32[2]{0:T(128)} %pad_add_fusion.pos_ref, s32[4,1200]{1,0:T(4,128)} %box_ref.3, f32[8,1408]{1,0:T(8,128)} %select_maximum_fusion.seg_ref, bf16[8,2,128,128]{3,2,1,0:T(8,128)(2,1)} %all_to_all.26.h_ref, bf16[512,8192]{1,0:T(8,128)(2,1)} %get-tuple-element.9.x_ref, f32[16,8192]{1,0:T(8,128)} %get-tuple-element.10.across_ref), custom_call_target="tpu_custom_call" | custom-call | tf_op jit(solution)/shard_map/weight/pallas_call | solution.py:472
  93.1 0.8 all_to_all.21
  93.9 15.0 %all_to_all.27 = f32[32,1,192]{2,1,0:T(1,128)S(1)} all-to-all(f32[32,1,192]{2,1,0:T(1,128)S(1)} %all_to_all.21), channel_id=1, replica_groups=mesh['band'=4,'row'=8] {'band','row'}, dimensions={0} | all-to-all | bytes 49152 | tf_op jit(solution)/shard_map/all_to_all | solution.py:508
  108.9 0.1 reduce_sum.9
  109.0 8.9 %all_to_all.28 = f32[32,1,192]{2,1,0:T(1,128)S(1)} all-to-all(f32[32,1,192]{2,1,0:T(1,128)S(1)} %broadcast_in_dim.2), channel_id=1, replica_groups=mesh['band'=4,'row'=8] {'band','row'}, dimensions={0} | all-to-all | bytes 49152 | tf_op jit(solution)/shard_map/all_to_all | solution.py:510
  117.9 0.1 reduce.1
  118.0 0.1 reshape.21
  118.1 0.7 reshape.22
  (1 shorter events, 0.0 us)
Async XLA Ops:
  23.3 21.7 %all-to-all-start = ((bf16[8,2,128,128]{3,2,1,0:T(8,128)(2,1)}), bf16[8,2,128,128]{3,2,1,0:T(8,128)(2,1)S(1)}, u32[]{:S(2)}, u32[]{:S(2)}) async-start(bf16[8,2,128,128]{3,2,1,0:T(8,128)(2,1)} %get-tuple-element.8), calls=%async_computation | async-start | bytes 1048576 | tf_op jit(solution)/shard_map/all_to_all | solution.py:444
  45.0 0.9 copy-start
where the time goes:
time: 120 us; the launch traced here: 119 us
  Pallas kernels  48.3 us (40%)
  blocking collectives  43.4 us (36%)
  waiting for transfers between devices  12 us (10%)
  starting transfers between devices  6.37 us (5%)
  other arithmetic  4.72 us (4%)
  local copies, waits for them, and re-layouts  3.9 us (3%)
    pallas_call x1, Pallas kernels, body(): pl.pallas_call(functools.partial(weight_kernel, (rows, cols, block, bands...  24.2 us
    pallas_call x1, Pallas kernels, body(): pl.pallas_call(functools.partial(field_kernel, (rows, cols, block, bands,...  20.6 us
    all_to_all x1, blocking collectives, body(): lax.all_to_all(spread, 'row', split_axis=0, concat_axis=0, tiled=True)  19.5 us
    all_to_all x1, blocking collectives, body(): lax.all_to_all(shares, axes, split_axis=0, concat_axis=0, tiled=True)  15 us
    all_to_all x1, waiting for transfers between devices, body(): lax.all_to_all(half_way, 'row', split_axis=0, concat_axis=0, tiled=True)  12 us
    all_to_all x1, blocking collectives, body(): lax.all_to_all(copies, axes, split_axis=0, concat_axis=0, tiled=True)  8.94 us
    all_to_all x1, starting transfers between devices, body(): lax.all_to_all(half_way, 'row', split_axis=0, concat_axis=0, tiled=True)  6.37 us
    pallas_call x1, Pallas kernels, body(): pl.pallas_call(functools.partial(focal_kernel, (rows, cols, bands, focal,...  3.43 us
  transfers between devices with their start and end apart: 1, of which 1 were waited for; matrix products, arithmetic and copies ran while one was open for 3% of the time, Pallas kernels for 0%

commit v1 on v0

v1 whole, which is shorter than its diff:
```python
import functools
import math

import jax
import jax.numpy as jnp
from jax import lax
from jax.experimental import pallas as pl
from jax.experimental.pallas import tpu as pltpu
from jax.sharding import PartitionSpec as P

SROWS = 16
SAMPLING = 0.5
SPREAD = 0.2
TWO_PI = 2.0 * math.pi
LANES = 128
F32 = jnp.float32
BF16 = jnp.bfloat16

SIN_HALF = (0.9999999971, -0.1666666029, 0.008333109246, -0.0001981365728, 2.616271295e-06)
COS_HALF = (0.9999999682, -0.4999993032, 0.04166421727, -0.001385868782, 2.327410856e-05)
SIN_WAVE = (0.9999999964, -0.166666488, 0.008331936401, -0.000194912576)
COS_WAVE = (0.9999999679, -0.499998396, 0.04165412354, -0.001357443708)
SIN_TURN = (
    6.283185307, -41.34170222, 81.60524741, -76.70580003,
    42.05775188, -15.08655272, 3.781282403, -0.6207370354,
)
COS_TURN = (
    0.9999999999, -19.73920874, 64.93938905, -85.45665775,
    60.24212493, -26.40463062, 7.800022219, -1.452987552,
)


def series(coeffs, t):
    value = jnp.full_like(t, coeffs[-1])
    for c in reversed(coeffs[:-1]):
        value = value * t + c
    return value


def turn_cos_sin(turns):
    t = turns - jnp.floor(turns + 0.5)
    square = t * t
    return series(COS_TURN, square), t * series(SIN_TURN, square)


def iota(shape, axis):
    return lax.broadcasted_iota(jnp.int32, shape, axis)


def focal_scale(m_positive, band, band_total):
    ratio = 1.0 + SPREAD * ((band.astype(F32) + 0.5) / band_total - 0.5)
    return m_positive / ratio


def band_lanes(first_band, bands, half, band_total, rows):
    pieces = []
    for b in range(bands):
        q = (iota((rows, half), 1).astype(F32) + 0.5) * SAMPLING
        band = jnp.full((rows, half), 1, jnp.int32) * (first_band + b)
        pieces.append(focal_scale(q, band, band_total))
    return jnp.concatenate(pieces, axis=1)


def column_tables(first_band, bands, half, band_total, cols, tile_ref, shift_ref):
    q = band_lanes(first_band, bands, half, band_total, LANES)
    c, s = turn_cos_sin(q * (iota(q.shape, 0).astype(F32) / cols))
    tile_ref[0] = c
    tile_ref[1] = s
    tiles = cols // (2 * LANES)
    q = band_lanes(first_band, bands, half, band_total, tiles)
    x = (iota(q.shape, 0).astype(F32) * LANES + 0.5) / cols - 0.5
    c, s = turn_cos_sin(q * x)
    shift_ref[0] = c
    shift_ref[1] = s


def write_table(cos_ref, sin_ref, tile_ref, shift_ref, first_tile, tiles):
    for i in range(tiles):
        sc = shift_ref[0, pl.ds(first_tile + i, 1), :]
        ss = shift_ref[1, pl.ds(first_tile + i, 1), :]
        for k in range(0, LANES, 16):
            tc = tile_ref[0, k : k + 16]
            ts = tile_ref[1, k : k + 16]
            rows = slice(i * LANES + k, i * LANES + k + 16)
            cos_ref[rows] = (tc * sc - ts * ss).astype(BF16)
            sin_ref[rows] = (ts * sc + tc * ss).astype(BF16)


def load_segments(coeffs_ref, boxes_ref, seg_ref):
    seg_ref[...] = jnp.zeros_like(seg_ref)
    seg_ref[0:3, : coeffs_ref.shape[1]] = coeffs_ref[...]
    seg_ref[3:7, : boxes_ref.shape[1]] = boxes_ref[...].astype(F32)


def reverse(x):
    back = LANES - 1 - iota((8, LANES), 1)
    pieces = [gather_lanes(x[k : k + 8], back) for k in range(0, x.shape[0], 8)]
    return pieces[0] if len(pieces) == 1 else jnp.concatenate(pieces, axis=0)


def gather_lanes(x, index):
    return jnp.take_along_axis(x, index, axis=1, mode="promise_in_bounds")


def tile_row_pieces(seg_ref, per_row, width):
    for t in range(SROWS):
        yield t, pltpu.roll(seg_ref[...], (width - t * per_row) % width, axis=1)[:, :LANES]


def field_kernel(
    dims, pos_ref, box_ref, freq_ref, amp_ref, coeffs_ref, boxes_ref,
    amplitude_ref, amplitude_far_ref, map_ref, map_far_ref,
    x_ref, across_ref, index_ref, y_ref,
    seg_ref, tables, bases, slot_tables, waves, tile_ref, shift_ref, cos_ref, sin_ref,
    even_ref, odd_ref, total_ref, slot_map,
):
    rows, cols, block, bands, half, band_total, total_rows, per_row, pairs, vloc, owners = dims
    step = pl.program_id(0)
    row0 = pos_ref[0] * rows
    chunks = block // LANES
    maps = (map_ref, map_far_ref)
    amplitudes = (amplitude_ref, amplitude_far_ref)

    @pl.when(step == 0)
    def _():
        load_segments(coeffs_ref, boxes_ref, seg_ref)
        width = seg_ref.shape[1]
        groups = rows // 8
        values = [[jnp.zeros((8, LANES), F32)] * 4 for _ in range(groups)]
        base = [jnp.zeros((8, LANES), jnp.int32)] * groups
        for t, piece in tile_row_pieces(seg_ref, per_row, width):
            part = [jnp.broadcast_to(piece[k : k + 1], (8, LANES)) for k in range(7)]
            low, high = part[3][:, :1], part[4][:, :1]
            mid_row = 0.5 * (part[3] + part[4])
            inv_row = 1.0 / (part[4] - part[3] + 1.0)
            slope, mid = 0.5 * part[1], 0.5 * (part[5] + part[6])
            inv = 2.0 / (part[6] - part[5] + 1.0)
            slot_tables[0, t : t + 1] = mid[:1]
            slot_tables[1, t : t + 1] = inv[:1]
            for g in range(groups):
                here = (row0 + g * 8 + iota((8, LANES), 0)).astype(F32)
                mine = (here >= low) & (here <= high)
                new = (0.5 * part[0] + part[2] * ((here - mid_row) * inv_row), slope, mid, inv)
                values[g] = [jnp.where(mine, n, v) for n, v in zip(new, values[g])]
                base[g] = jnp.where(mine, t * per_row, base[g])
        for g in range(groups):
            for k in range(4):
                tables[k, g * 8 : (g + 1) * 8] = values[g][k]
            bases[g * 8 : (g + 1) * 8] = base[g]
        y = ((row0 + iota((rows, LANES), 0)).astype(F32) + 0.5) / cols - total_rows / (2.0 * cols)
        for j in range(pairs):
            c, s = turn_cos_sin(freq_ref[j, 1].astype(F32) * y)
            waves[2 * j] = amp_ref[j] * c
            waves[2 * j + 1] = amp_ref[j] * s
        column_tables(pos_ref[1] * bands, bands, half, band_total, cols, tile_ref, shift_ref)
        total_ref[...] = jnp.zeros_like(total_ref)

    row = iota((8, block), 0)
    freq = jnp.zeros((8, block), F32)
    for j in range(pairs):
        freq = jnp.where(row // 2 == j, freq_ref[j, 0].astype(F32), freq)
    x = ((iota((8, block), 1) + step * block).astype(F32) + 0.5) / cols - 0.5
    turn_c, turn_s = turn_cos_sin(freq * x)
    columns_wave = jnp.where(row % 2 == 0, turn_s, turn_c)

    for t in range(SROWS):
        first = jnp.clip(box_ref[0, t * per_row] - row0, 0, rows - 1)
        for side in range(2):
            slot_map[side, t : t + 1, :] = maps[side][pl.ds(first, 1), :] - t * per_row

    write_table(cos_ref, sin_ref, tile_ref, shift_ref, step * chunks, chunks)

    for i in range(chunks):
        lanes = slice(i * LANES, (i + 1) * LANES)
        far_lanes = slice((chunks - 1 - i) * LANES, (chunks - i) * LANES)
        near_column = (iota((16, LANES), 1) + (step * block + i * LANES)).astype(F32)
        columns = (near_column, (cols - 1.0) - near_column)
        for side in range(2):
            for t in range(0, SROWS, 8):
                index = slot_map[side, t : t + 8, far_lanes if side else lanes] & (LANES - 1)
                if side:
                    index = reverse(index)
                mid = gather_lanes(slot_tables[0, t : t + 8], index)
                inv = gather_lanes(slot_tables[1, t : t + 8], index)
                across_ref[side, t : t + 8, lanes] = (columns[side][:8] - mid) * inv
                index_ref[side, t : t + 8, lanes] = index
        for g in range(0, rows, 16):
            here = slice(g, g + 16)
            fields = []
            for side in range(2):
                source = far_lanes if side else lanes
                index = maps[side][here, source] - bases[here]
                size = amplitudes[side][here, source].astype(F32)
                if side:
                    index, size = reverse(index), reverse(size)

                def pick(k):
                    return jnp.concatenate(
                        [
                            gather_lanes(tables[k, g + h : g + h + 8], index[h : h + 8])
                            for h in (0, 8)
                        ],
                        axis=0,
                    )

                half_phase = pick(0) + pick(1) * ((columns[side] - pick(2)) * pick(3))
                square = half_phase * half_phase
                s = half_phase * series(SIN_HALF, square)
                c = series(COS_HALF, square)
                twice = s + s
                fields.append((size * (1.0 - twice * s), size * (twice * c)))
            for j in range(pairs):
                from_sin = columns_wave[2 * j : 2 * j + 1, lanes] * waves[2 * j, here]
                from_cos = columns_wave[2 * j + 1 : 2 * j + 2, lanes] * waves[2 * j + 1, here]
                parts = []
                for wave in (from_cos + from_sin, from_cos - from_sin):
                    square = wave * wave
                    parts.append((series(COS_WAVE, square), wave * series(SIN_WAVE, square)))
                for k in range(2):
                    for o in range(2):
                        at = (4 * j + 2 * k + o) * rows + g
                        near = fields[0][o] * parts[0][k]
                        far = fields[1][o] * parts[1][k]
                        x_ref[0, at : at + 16, lanes] = near.astype(BF16)
                        x_ref[1, at : at + 16, lanes] = far.astype(BF16)
                        even_ref[at : at + 16, lanes] = (near + far).astype(BF16)
                        odd_ref[at : at + 16, lanes] = (near - far).astype(BF16)

    total_ref[0] += jnp.dot(even_ref[...], cos_ref[...], preferred_element_type=F32)
    total_ref[1] += jnp.dot(odd_ref[...], sin_ref[...], preferred_element_type=F32)

    @pl.when(step == pl.num_programs(0) - 1)
    def _():
        r2 = 2 * rows
        m = iota((half, half), 0)
        n = iota((half, half), 1)
        straight = (m == n).astype(F32).astype(BF16)
        turned = (m + n == half - 1).astype(F32).astype(BF16)
        nt = (((1,), (1,)), ((), ()))
        for b in range(bands):
            for p in range(2 * pairs):
                cos_part = total_ref[0, p * r2 : (p + 1) * r2, b * half : (b + 1) * half]
                sin_part = total_ref[1, p * r2 : (p + 1) * r2, b * half : (b + 1) * half]
                swapped = jnp.concatenate([sin_part[rows:], -sin_part[:rows]], axis=0)
                low = lax.dot_general(
                    turned, (cos_part - swapped).astype(BF16), nt, preferred_element_type=F32
                ).astype(BF16)
                high = lax.dot_general(
                    straight, (cos_part + swapped).astype(BF16), nt, preferred_element_type=F32
                ).astype(BF16)
                if owners:
                    each = half // vloc
                    for d in range(each):
                        piece = slice(d * vloc, (d + 1) * vloc)
                        y_ref[d, b, p * vloc : (p + 1) * vloc, :] = low[piece]
                        y_ref[each + d, b, p * vloc : (p + 1) * vloc, :] = high[piece]
                else:
                    y_ref[b, p, :half, :] = low
                    y_ref[b, p, half:, :] = high


def focal_kernel(dims, pos_ref, y_ref, measured_ref, h_ref, table_ref):
    rows, cols, bands, focal, band_total, total_rows, sources, scale = dims
    r2 = 2 * rows
    for b in range(bands):
        band = jnp.full((rows, focal), 1, jnp.int32) * (pos_ref[1] * bands + b)
        q = (iota((rows, focal), 1).astype(F32) + (0.5 - focal / 2)) * SAMPLING
        q = focal_scale(q, band, band_total)
        tile_c, tile_s = turn_cos_sin(q * (iota(q.shape, 0).astype(F32) / cols))
        first = iota((sources, focal), 0).astype(F32) * rows + 0.5
        y = first / cols - total_rows / (2.0 * cols)
        shift_c, shift_s = turn_cos_sin(jnp.broadcast_to(q[:1], y.shape) * y)
        for d in range(sources):
            sc, ss = shift_c[d : d + 1], shift_s[d : d + 1]
            c = (tile_c * sc - tile_s * ss).astype(BF16)
            s_value = tile_s * sc + tile_c * ss
            s = s_value.astype(BF16)
            table_ref[d * r2 : d * r2 + rows, :focal] = c
            table_ref[d * r2 : d * r2 + rows, focal:] = (-s_value).astype(BF16)
            table_ref[d * r2 + rows : (d + 1) * r2, :focal] = s
            table_ref[d * r2 + rows : (d + 1) * r2, focal:] = c
        lhs = jnp.concatenate([y_ref[d, b] for d in range(sources)], axis=1)
        f = jnp.dot(lhs, table_ref[...], preferred_element_type=F32)
        residual = (f * (2.0 * scale) - measured_ref[b]).astype(BF16)
        spread = lax.dot_general(
            residual, table_ref[...], (((1,), (1,)), ((), ())), preferred_element_type=F32
        )
        for d in range(sources):
            h_ref[d, b] = spread[:, d * r2 : (d + 1) * r2].astype(BF16)


def weight_kernel(
    dims, pos_ref, box_ref, h_ref, x_ref, across_ref, index_ref, out_ref,
    left_ref, pick_ref, tile_ref, shift_ref, cos_ref, sin_ref, p_ref, q_ref, weight_ref, sums_ref,
    term_ref,
):
    rows, cols, block, bands, half, band_total, per_row, pairs, vloc, sources, scale = dims
    step = pl.program_id(0)
    row0 = pos_ref[0] * rows
    r2 = 2 * rows
    nt = (((1,), (1,)), ((), ()))

    @pl.when(step == 0)
    def _():
        column_tables(pos_ref[1] * bands, bands, half, band_total, cols, tile_ref, shift_ref)
        m = iota((half, 2 * half), 0)
        v = iota((half, 2 * half), 1)
        upper = (v == half + m).astype(F32)
        lower = (v == half - 1 - m).astype(F32)
        even, odd = (upper + lower).astype(BF16), (upper - lower).astype(BF16)
        same = (iota((r2, r2), 0) == iota((r2, r2), 1)).astype(F32).astype(BF16)
        for b in range(bands):
            for p in range(2 * pairs):
                if sources:
                    block_h = jnp.concatenate(
                        [h_ref[d, b, p * vloc : (p + 1) * vloc, :] for d in range(sources)], axis=0
                    )
                else:
                    block_h = h_ref[b, p]

                def fold(mirror):
                    folded = jnp.dot(mirror, block_h, preferred_element_type=F32).astype(BF16)
                    return lax.dot_general(same, folded, nt, preferred_element_type=F32)

                plus, minus = fold(even), fold(odd)
                at = slice(p * r2, (p + 1) * r2)
                left_ref[0, at, b * half : (b + 1) * half] = plus.astype(BF16)
                left_ref[1, at, b * half : (b + 1) * half] = jnp.concatenate(
                    [-minus[rows:], minus[:rows]], axis=0
                ).astype(BF16)
        slot = iota((SROWS, r2), 0)
        lane = iota((SROWS, r2), 1)
        here = (row0 + lane % rows).astype(F32)
        low = jnp.zeros((SROWS, r2), F32)
        high = jnp.zeros((SROWS, r2), F32)
        for t in range(SROWS):
            low = jnp.where(slot == t, box_ref[0, t * per_row].astype(F32), low)
            high = jnp.where(slot == t, box_ref[1, t * per_row].astype(F32), high)
        mine = ((here >= low) & (here <= high)).astype(F32)
        down = mine * ((here - 0.5 * (low + high)) / (0.5 * (high - low + 1.0)))
        down_high = down.astype(BF16)
        pick_ref[:SROWS] = mine.astype(BF16)
        pick_ref[SROWS : 2 * SROWS] = down_high
        pick_ref[2 * SROWS :] = (down - down_high.astype(F32)).astype(BF16)
        out_ref[...] = jnp.zeros_like(out_ref)

    chunks = block // LANES
    write_table(cos_ref, sin_ref, tile_ref, shift_ref, step * chunks, chunks)
    p_ref[...] = lax.dot_general(left_ref[0], cos_ref[...], nt, preferred_element_type=F32)
    q_ref[...] = lax.dot_general(left_ref[1], sin_ref[...], nt, preferred_element_type=F32)
    for i in range(chunks):
        lanes = slice(i * LANES, (i + 1) * LANES)
        for g in range(0, rows, 16):
            near = jnp.zeros((16, LANES), F32)
            far = jnp.zeros((16, LANES), F32)
            for p in range(2 * pairs):
                re = slice(p * r2 + g, p * r2 + g + 16)
                im = slice(p * r2 + rows + g, p * r2 + rows + g + 16)
                p_re, p_im, q_re, q_im = p_ref[re, lanes], p_ref[im, lanes], q_ref[re, lanes], q_ref[im, lanes]
                near = near + (
                    x_ref[0, re, lanes].astype(F32) * (p_im + q_im)
                    - x_ref[0, im, lanes].astype(F32) * (p_re + q_re)
                )
                far = far + (
                    x_ref[1, re, lanes].astype(F32) * (p_im - q_im)
                    - x_ref[1, im, lanes].astype(F32) * (p_re - q_re)
                )
            for side, value in enumerate((near, far)):
                high = value.astype(BF16)
                to = slice(side * block + i * LANES, side * block + (i + 1) * LANES)
                weight_ref[g : g + 16, to] = high
                weight_ref[rows + g : rows + g + 16, to] = (value - high.astype(F32)).astype(BF16)
    sums = jnp.dot(pick_ref[...], weight_ref[...], preferred_element_type=F32)
    for side in range(2):
        mine = sums[:, side * block : (side + 1) * block]
        sums_ref[step, side, 0] = mine[:SROWS]
        sums_ref[step, side, 1] = mine[:SROWS] * across_ref[side]
        sums_ref[step, side, 2] = mine[SROWS : 2 * SROWS] + mine[2 * SROWS :]
        term_ref[step, side] = index_ref[side]

    @pl.when(step == pl.num_programs(0) - 1)
    def _():
        tops = [box_ref[0, t * per_row] for t in range(SROWS)]
        bottoms = [box_ref[1, t * per_row] for t in range(SROWS)]
        first = sum((bottom < row0).astype(jnp.int32) for bottom in bottoms)
        last = sum((top < row0 + rows).astype(jnp.int32) for top in tops)

        def tile_row(t, carry):
            def add(i, total):
                for side in range(2):
                    index = term_ref[i, side, pl.ds(t, 1), :]
                    inside = (iota((LANES, block), 0) == index).astype(F32).astype(BF16)
                    terms = [sums_ref[i, side, q, pl.ds(t, 1), :] for q in range(3)]
                    highs = [x.astype(BF16).astype(F32) for x in terms]
                    lows = [x - h for x, h in zip(terms, highs)]
                    stacked = jnp.concatenate(highs + lows + lows[:2], axis=0).astype(BF16)
                    total = total + lax.dot_general(
                        stacked, inside, nt, preferred_element_type=F32
                    )
                return total

            total = lax.fori_loop(0, pl.num_programs(0), add, jnp.zeros((8, LANES), F32))
            for q in range(3):
                out_ref[q, pl.ds(t, 1)] = (total[q : q + 1] + total[q + 3 : q + 4]) * scale
            return carry

        lax.fori_loop(first, last, tile_row, 0)


def body(amplitude, seg_map, seg_box, seg_coeffs, probe_freq, probe_amp, measured):
    rows, cols = amplitude.shape
    owners = lax.axis_size("row")
    band_axis = lax.axis_size("band")
    total_rows = rows * owners
    bands, vloc, probes, _, focal = measured.shape
    pairs = probes // 2
    half = focal // 2
    band_total = bands * band_axis
    segments = seg_coeffs.shape[1]
    per_row = segments // SROWS
    arrays = 2 * pairs
    r2 = 2 * rows
    normf = 1.0 / math.sqrt(total_rows * cols)
    aligned = vloc % 16 == 0
    block = 512
    blocks = cols // block
    steps = blocks // 2

    pos = jnp.stack([lax.axis_index("row"), lax.axis_index("band")]).astype(jnp.int32)
    width = -(-(segments + LANES) // LANES) * LANES
    smem = pl.BlockSpec(memory_space=pltpu.SMEM)
    whole = pl.BlockSpec(memory_space=pltpu.VMEM)
    k_width = bands * half

    def resident(shape):
        return pl.BlockSpec(shape, lambda i: (0,) * len(shape), pipeline_mode=pl.Buffered(1))

    near = pl.BlockSpec((rows, block), lambda i: (0, i))
    far = pl.BlockSpec((rows, block), lambda i: (0, blocks - 1 - i))
    x_spec = pl.BlockSpec((2, arrays * r2, block), lambda i: (0, 0, i))
    slot_spec = pl.BlockSpec((2, SROWS, block), lambda i: (0, 0, i))
    y_shape = (owners, bands, arrays * vloc, r2) if aligned else (bands, arrays, focal, r2)
    fields, across, index, half_way = pl.pallas_call(
        functools.partial(
            field_kernel,
            (rows, cols, block, bands, half, band_total, total_rows, per_row, pairs, vloc, aligned),
        ),
        grid=(steps,),
        in_specs=[
            smem, smem, smem, smem,
            resident(seg_coeffs.shape),
            resident(seg_box.shape),
            near, far, near, far,
        ],
        out_specs=[
            x_spec,
            slot_spec,
            slot_spec,
            pl.BlockSpec(y_shape, lambda i: (0,) * len(y_shape)),
        ],
        out_shape=[
            jax.ShapeDtypeStruct((2, arrays * r2, cols // 2), BF16),
            jax.ShapeDtypeStruct((2, SROWS, cols // 2), F32),
            jax.ShapeDtypeStruct((2, SROWS, cols // 2), jnp.int32),
            jax.ShapeDtypeStruct(y_shape, BF16),
        ],
        scratch_shapes=[
            pltpu.VMEM((8, width), F32),
            pltpu.VMEM((4, rows, LANES), F32),
            pltpu.VMEM((rows, LANES), jnp.int32),
            pltpu.VMEM((2, SROWS, LANES), F32),
            pltpu.VMEM((2 * pairs, rows, LANES), F32),
            pltpu.VMEM((2, LANES, k_width), F32),
            pltpu.VMEM((2, cols // (2 * LANES), k_width), F32),
            pltpu.VMEM((block, k_width), BF16),
            pltpu.VMEM((block, k_width), BF16),
            pltpu.VMEM((arrays * r2, block), BF16),
            pltpu.VMEM((arrays * r2, block), BF16),
            pltpu.VMEM((2, arrays * r2, k_width), F32),
            pltpu.VMEM((2, SROWS, block), jnp.int32),
        ],
        compiler_params=pltpu.CompilerParams(dimension_semantics=("arbitrary",)),
        name="field",
    )(pos, seg_box, probe_freq, probe_amp, seg_coeffs, seg_box,
      amplitude, amplitude, seg_map, seg_map)

    if not aligned:
        half_way = (
            half_way.reshape(bands, arrays, owners, vloc, r2)
            .transpose(2, 0, 1, 3, 4)
            .reshape(owners, bands, arrays * vloc, r2)
        )
    regrouped = lax.all_to_all(half_way, "row", split_axis=0, concat_axis=0, tiled=True)

    plus, minus = measured[:, :, 0::2], measured[:, :, 1::2]
    total, difference = plus + minus, plus - minus
    turned = jnp.stack([difference[:, :, :, 1], -difference[:, :, :, 0]], axis=3)
    targets = jnp.stack([total, turned], axis=3)
    targets = targets.transpose(0, 2, 3, 1, 4, 5).reshape(bands, arrays * vloc, 2 * focal)

    spread = pl.pallas_call(
        functools.partial(
            focal_kernel, (rows, cols, bands, focal, band_total, total_rows, owners, normf)
        ),
        in_specs=[smem, whole, whole],
        out_specs=whole,
        out_shape=jax.ShapeDtypeStruct((owners, bands, arrays * vloc, r2), BF16),
        scratch_shapes=[pltpu.VMEM((owners * r2, 2 * focal), BF16)],
        name="focal",
    )(pos, regrouped, targets)

    hidden = lax.all_to_all(spread, "row", split_axis=0, concat_axis=0, tiled=True)
    if not aligned:
        hidden = (
            hidden.reshape(owners, bands, arrays, vloc, r2)
            .transpose(1, 2, 0, 3, 4)
            .reshape(bands, arrays, focal, r2)
        )

    scale = 2.0 * normf / (band_total * probes)
    local = pl.pallas_call(
        functools.partial(
            weight_kernel,
            (
                rows, cols, block, bands, half, band_total, per_row, pairs, vloc,
                owners if aligned else 0, scale,
            ),
        ),
        grid=(steps,),
        in_specs=[smem, smem, resident(hidden.shape), x_spec, slot_spec, slot_spec],
        out_specs=pl.BlockSpec((3, SROWS, LANES), lambda i: (0, 0, 0)),
        out_shape=jax.ShapeDtypeStruct((3, SROWS, LANES), F32),
        scratch_shapes=[
            pltpu.VMEM((2, arrays * r2, k_width), BF16),
            pltpu.VMEM((3 * SROWS, r2), BF16),
            pltpu.VMEM((2, LANES, k_width), F32),
            pltpu.VMEM((2, cols // (2 * LANES), k_width), F32),
            pltpu.VMEM((block, k_width), BF16),
            pltpu.VMEM((block, k_width), BF16),
            pltpu.VMEM((arrays * r2, block), F32),
            pltpu.VMEM((arrays * r2, block), F32),
            pltpu.VMEM((r2, 2 * block), BF16),
            pltpu.VMEM((steps, 2, 3, SROWS, block), F32),
            pltpu.VMEM((steps, 2, SROWS, block), jnp.int32),
        ],
        compiler_params=pltpu.CompilerParams(dimension_semantics=("arbitrary",)),
        name="weight",
    )(pos, seg_box, hidden, fields, across, index)

    devices = owners * band_axis
    axes = ("band", "row")
    shares = local.reshape(devices, -1)
    mine = jnp.sum(lax.all_to_all(shares, axes, split_axis=0, concat_axis=0, tiled=True), axis=0)
    copies = jnp.broadcast_to(mine[None], shares.shape)
    gathered = lax.all_to_all(copies, axes, split_axis=0, concat_axis=0, tiled=True)
    return gathered.reshape(3, SROWS, LANES)[:, :, :per_row].reshape(3, segments)


def solution(mesh):
    in_specs = (
        P("row", None),
        P("row", None),
        P(),
        P(),
        P(),
        P(),
        P("band", "row", None, None, None),
    )
    return jax.shard_map(body, mesh=mesh, in_specs=in_specs, out_specs=P(), check_vma=False)
```

time: 120 us -> 105 us (0.88)
  Pallas kernels: 48.3 us -> 40.4 us
  blocking collectives: 43.4 us -> 39 us
  other arithmetic: 4.72 us -> 2.62 us
    pallas_call x1, Pallas kernels: 24.2 us -> 17 us  [body(): pl.pallas_call(functools.partial(weight_kernel, (rows, cols, block, bands...]
    all_to_all x1, blocking collectives: 15 us -> 10.6 us  [body(): lax.all_to_all(shares, axes, split_axis=0, concat_axis=0, tiled=True)]
    concatenate x1 -> x0, other arithmetic: 1.36 us -> none  [body(): jnp.concatenate([seg_coeffs, seg_box.astype(F32)], axis=0)]
where the time goes in v1:
time: 105 us; the launch traced here: 104 us
  Pallas kernels  40.4 us (38%)
  blocking collectives  39 us (37%)
  waiting for transfers between devices  12 us (11%)
  starting transfers between devices  6.35 us (6%)
  local copies, waits for them, and re-layouts  3.82 us (4%)
  other arithmetic  2.62 us (2%)
    pallas_call x1, Pallas kernels, body(): pl.pallas_call(functools.partial(field_kernel, (rows, cols, block, bands,...  19.9 us
    all_to_all x1, blocking collectives, body(): lax.all_to_all(spread, 'row', split_axis=0, concat_axis=0, tiled=True)  19.5 us
    pallas_call x1, Pallas kernels, body(): pl.pallas_call(functools.partial(weight_kernel, (rows, cols, block, bands...  17 us
    all_to_all x1, waiting for transfers between devices, body(): lax.all_to_all(half_way, 'row', split_axis=0, concat_axis=0, tiled=True)  12 us
    all_to_all x1, blocking collectives, body(): lax.all_to_all(shares, axes, split_axis=0, concat_axis=0, tiled=True)  10.6 us
    all_to_all x1, blocking collectives, body(): lax.all_to_all(copies, axes, split_axis=0, concat_axis=0, tiled=True)  8.94 us
    all_to_all x1, starting transfers between devices, body(): lax.all_to_all(half_way, 'row', split_axis=0, concat_axis=0, tiled=True)  6.35 us
    pallas_call x1, Pallas kernels, body(): pl.pallas_call(functools.partial(focal_kernel, (rows, cols, bands, focal,...  3.48 us
  transfers between devices with their start and end apart: 1, of which 1 were waited for; matrix products, arithmetic and copies ran while one was open for 3% of the time, Pallas kernels for 0%

profile of v1, /device:TPU:0, one launch (start us, length us, event | category | flops | bytes accessed | tf_op | source)
XLA Modules:
  0.0 104.2 jit_solution(8172622405582260)
XLA Ops:
  0.0 0.6 pad_add_fusion.pos_ref
  0.6 19.9 %field.1 = (bf16[2,512,4096]{2,1,0:T(8,128)(2,1)}, f32[2,16,4096]{2,1,0:T(8,128)}, s32[2,16,4096]{2,1,0:T(8,128)}, bf16[8,2,128,128]{3,2,1,0:T(8,128)(2,1)}) custom-call(s32[2]{0:T(128)} %pad_add_fusion.pos_ref, s32[4,1200]{1,0:T(4,128)} %box_ref.3, s32[2,2]{1,0:T(2,128)} %freq_ref.1, f32[2]{0:T(128)} %amp_ref.1, f32[3,1200]{1,0:T(4,128)} %coeffs_ref.1, ...), custom_call_target="tpu_custom_call" | custom-call | tf_op jit(solution)/shard_map/field/pallas_call | solution.py:443
  20.5 6.4 %all-to-all-start = ((bf16[8,2,128,128]{3,2,1,0:T(8,128)(2,1)}), bf16[8,2,128,128]{3,2,1,0:T(8,128)(2,1)S(1)}, u32[]{:S(2)}, u32[]{:S(2)}) async-start(bf16[8,2,128,128]{3,2,1,0:T(8,128)(2,1)} %get-tuple-element.9), calls=%async_computation | async-start | bytes 1048576 | tf_op jit(solution)/shard_map/all_to_all | solution.py:493
  26.9 1.2 %add_bitcast_fusion = (f32[2,32,2,1,2,256]{5,4,2,1,0,3:T(2,128)S(1)}, f32[2,32,2,2,256]{4,3,2,1,0:T(2,128)S(1)}) fusion(f32[2,32,4,2,256]{4,3,2,1,0:T(2,128)} %param.13), kind=kLoop, calls=%fused_computation.2 | loop fusion | flops 131072 | bytes 1048576 | tf_op jit(solution)/shard_map/stack | solution.py:498
  28.1 0.2 fusion
  28.3 0.2 maximum_bitcast_fusion.1
  28.5 0.2 maximum_bitcast_fusion
  28.8 0.2 copy.9
  29.0 1.2 %reshape.20.measured_ref = f32[2,128,512]{2,1,0:T(8,128)} reshape(f32[2,2,2,32,2,256]{5,4,3,2,1,0:T(2,128)S(1)} %copy.9) | data formatting | bytes 1048576 | tf_op jit(solution)/shard_map/reshape | solution.py:499
  30.2 12.0 %all-to-all-done.y_ref = bf16[8,2,128,128]{3,2,1,0:T(8,128)(2,1)S(1)} async-done(((bf16[8,2,128,128]{3,2,1,0:T(8,128)(2,1)}), bf16[8,2,128,128]{3,2,1,0:T(8,128)(2,1)S(1)}, u32[]{:S(2)}, u32[]{:S(2)}) %all-to-all-start) | async-done | bytes 524320 | tf_op jit(solution)/shard_map/all_to_all | solution.py:493
  42.2 0.0 copy-start
  42.2 0.8 copy-done
  43.0 3.5 %focal.1 = bf16[8,2,128,128]{3,2,1,0:T(8,128)(2,1)} custom-call(s32[2]{0:T(128)} %pad_add_fusion.pos_ref, bf16[8,2,128,128]{3,2,1,0:T(8,128)(2,1)} %copy-done, f32[2,128,512]{2,1,0:T(8,128)} %reshape.20.measured_ref), custom_call_target="tpu_custom_call" | custom-call | tf_op jit(solution)/shard_map/focal/pallas_call | solution.py:501
  46.5 19.5 %all_to_all.26.h_ref = bf16[8,2,128,128]{3,2,1,0:T(8,128)(2,1)} all-to-all(bf16[8,2,128,128]{3,2,1,0:T(8,128)(2,1)} %focal.1), channel_id=1, replica_groups=mesh['band'=4,'row'=8] {'row'}, dimensions={0} | all-to-all | bytes 1048576 | tf_op jit(solution)/shard_map/all_to_all | solution.py:512
  65.9 17.0 %weight.1 = f32[3,16,128]{2,1,0:T(8,128)} custom-call(s32[2]{0:T(128)} %pad_add_fusion.pos_ref, s32[4,1200]{1,0:T(4,128)} %box_ref.3, bf16[8,2,128,128]{3,2,1,0:T(8,128)(2,1)} %all_to_all.26.h_ref, bf16[2,512,4096]{2,1,0:T(8,128)(2,1)} %get-tuple-element.10.x_ref, f32[2,16,4096]{2,1,0:T(8,128)} %get-tuple-element.11.across_ref, ...), custom_call_target="tpu_custom_call" | custom-call | tf_op jit(solution)/shard_map/weight/pallas_call | solution.py:521
  82.9 0.8 all_to_all.21
  83.7 10.6 %all_to_all.27 = f32[32,1,192]{2,1,0:T(1,128)S(1)} all-to-all(f32[32,1,192]{2,1,0:T(1,128)S(1)} %all_to_all.21), channel_id=1, replica_groups=mesh['band'=4,'row'=8] {'band','row'}, dimensions={0} | all-to-all | bytes 49152 | tf_op jit(solution)/shard_map/all_to_all | solution.py:553
  94.3 0.1 reduce_sum.9
  94.4 8.9 %all_to_all.28 = f32[32,1,192]{2,1,0:T(1,128)S(1)} all-to-all(f32[32,1,192]{2,1,0:T(1,128)S(1)} %broadcast_in_dim.2), channel_id=1, replica_groups=mesh['band'=4,'row'=8] {'band','row'}, dimensions={0} | all-to-all | bytes 49152 | tf_op jit(solution)/shard_map/all_to_all | solution.py:555
  103.3 0.1 reduce.1
  103.4 0.1 reshape.21
  103.5 0.7 reshape.22
  (1 shorter events, 0.0 us)
Async XLA Ops:
  20.5 21.7 %all-to-all-start = ((bf16[8,2,128,128]{3,2,1,0:T(8,128)(2,1)}), bf16[8,2,128,128]{3,2,1,0:T(8,128)(2,1)S(1)}, u32[]{:S(2)}, u32[]{:S(2)}) async-start(bf16[8,2,128,128]{3,2,1,0:T(8,128)(2,1)} %get-tuple-element.9), calls=%async_computation | async-start | bytes 1048576 | tf_op jit(solution)/shard_map/all_to_all | solution.py:493
  42.2 0.8 copy-start

commit v2 on v1

v2 whole, which is shorter than its diff:
```python
import functools
import math

import jax
import jax.numpy as jnp
from jax import lax
from jax.experimental import pallas as pl
from jax.experimental.pallas import tpu as pltpu
from jax.sharding import PartitionSpec as P

SROWS = 16
SAMPLING = 0.5
SPREAD = 0.2
TWO_PI = 2.0 * math.pi
LANES = 128
F32 = jnp.float32
BLOCKS = (512, 2048, 512)
BF16 = jnp.bfloat16

SIN_HALF = (0.9999999971, -0.1666666029, 0.008333109246, -0.0001981365728, 2.616271295e-06)
COS_HALF = (0.9999999682, -0.4999993032, 0.04166421727, -0.001385868782, 2.327410856e-05)
SIN_WAVE = (0.9999999964, -0.166666488, 0.008331936401, -0.000194912576)
COS_WAVE = (0.9999999679, -0.499998396, 0.04165412354, -0.001357443708)
SIN_TURN = (
    6.283185307, -41.34170222, 81.60524741, -76.70580003,
    42.05775188, -15.08655272, 3.781282403, -0.6207370354,
)
COS_TURN = (
    0.9999999999, -19.73920874, 64.93938905, -85.45665775,
    60.24212493, -26.40463062, 7.800022219, -1.452987552,
)


def series(coeffs, t):
    value = jnp.full_like(t, coeffs[-1])
    for c in reversed(coeffs[:-1]):
        value = value * t + c
    return value


def turn_cos_sin(turns):
    t = turns - jnp.floor(turns + 0.5)
    square = t * t
    return series(COS_TURN, square), t * series(SIN_TURN, square)


def iota(shape, axis):
    return lax.broadcasted_iota(jnp.int32, shape, axis)


def focal_scale(m_positive, band, band_total):
    ratio = 1.0 + SPREAD * ((band.astype(F32) + 0.5) / band_total - 0.5)
    return m_positive / ratio


def band_lanes(first_band, bands, half, band_total, rows):
    pieces = []
    for b in range(bands):
        q = (iota((rows, half), 1).astype(F32) + 0.5) * SAMPLING
        band = jnp.full((rows, half), 1, jnp.int32) * (first_band + b)
        pieces.append(focal_scale(q, band, band_total))
    return jnp.concatenate(pieces, axis=1)


def column_tables(first_band, bands, half, band_total, cols, tile_ref, shift_ref):
    q = band_lanes(first_band, bands, half, band_total, LANES)
    c, s = turn_cos_sin(q * (iota(q.shape, 0).astype(F32) / cols))
    tile_ref[0] = c
    tile_ref[1] = s
    tiles = cols // (2 * LANES)
    q = band_lanes(first_band, bands, half, band_total, tiles)
    x = (iota(q.shape, 0).astype(F32) * LANES + 0.5) / cols - 0.5
    c, s = turn_cos_sin(q * x)
    shift_ref[0] = c
    shift_ref[1] = s


def write_table(cos_ref, sin_ref, tile_ref, shift_ref, first_tile, tiles):
    for i in range(tiles):
        sc = shift_ref[0, pl.ds(first_tile + i, 1), :]
        ss = shift_ref[1, pl.ds(first_tile + i, 1), :]
        for k in range(0, LANES, 16):
            tc = tile_ref[0, k : k + 16]
            ts = tile_ref[1, k : k + 16]
            rows = slice(i * LANES + k, i * LANES + k + 16)
            cos_ref[rows] = (tc * sc - ts * ss).astype(BF16)
            sin_ref[rows] = (ts * sc + tc * ss).astype(BF16)


def load_segments(coeffs_ref, boxes_ref, seg_ref):
    seg_ref[...] = jnp.zeros_like(seg_ref)
    seg_ref[0:3, : coeffs_ref.shape[1]] = coeffs_ref[...]
    seg_ref[3:7, : boxes_ref.shape[1]] = boxes_ref[...].astype(F32)


def reverse(x):
    back = LANES - 1 - iota((8, LANES), 1)
    pieces = [gather_lanes(x[k : k + 8], back) for k in range(0, x.shape[0], 8)]
    return pieces[0] if len(pieces) == 1 else jnp.concatenate(pieces, axis=0)


def gather_lanes(x, index):
    return jnp.take_along_axis(x, index, axis=1, mode="promise_in_bounds")


def tile_row_pieces(seg_ref, per_row, width):
    for t in range(SROWS):
        yield t, pltpu.roll(seg_ref[...], (width - t * per_row) % width, axis=1)[:, :LANES]


def probe_setup(pos_ref, freq_ref, amp_ref, j, rows, cols, total_rows, waves):
    row = pos_ref[0] * rows + iota((rows, LANES), 0)
    y = (row.astype(F32) + 0.5) / cols - total_rows / (2.0 * cols)
    c, s = turn_cos_sin(freq_ref[j, 1].astype(F32) * y)
    waves[2 * j] = amp_ref[j] * c
    waves[2 * j + 1] = amp_ref[j] * s


def column_wave(freq_ref, pairs, step, block, cols):
    row = iota((8, block), 0)
    freq = jnp.zeros((8, block), F32)
    for j in range(pairs):
        freq = jnp.where(row // 2 == j, freq_ref[j, 0].astype(F32), freq)
    x = ((iota((8, block), 1) + step * block).astype(F32) + 0.5) / cols - 0.5
    c, s = turn_cos_sin(freq * x)
    return jnp.where(row % 2 == 0, s, c)


def emit_pair(j, column, waves, fields, here, lanes, g, rows, x_ref, even_ref, odd_ref):
    from_sin = column[2 * j : 2 * j + 1, lanes] * waves[2 * j, here]
    from_cos = column[2 * j + 1 : 2 * j + 2, lanes] * waves[2 * j + 1, here]
    parts = []
    for wave in (from_cos + from_sin, from_cos - from_sin):
        square = wave * wave
        parts.append(
            (
                series(COS_WAVE, square).astype(BF16),
                (wave * series(SIN_WAVE, square)).astype(BF16),
            )
        )
    for k in range(2):
        for o in range(2):
            at = (2 * k + o) * rows + g
            near = fields[0][o] * parts[0][k]
            far = fields[1][o] * parts[1][k]
            x_ref[j, 0, at : at + 16, lanes] = near
            x_ref[j, 1, at : at + 16, lanes] = far
            at = at + 4 * j * rows
            even_ref[at : at + 16, lanes] = near + far
            odd_ref[at : at + 16, lanes] = near - far


def emit_half_way(pairs, total_ref, y_ref, rows, bands, half, vloc, owners):
    r2 = 2 * rows
    m = iota((half, half), 0)
    n = iota((half, half), 1)
    straight = (m == n).astype(F32).astype(BF16)
    turned = (m + n == half - 1).astype(F32).astype(BF16)
    nt = (((1,), (1,)), ((), ()))
    for b in range(bands):
        for p in range(2 * pairs):
            at = slice(p * r2, (p + 1) * r2)
            cos_part = total_ref[0, at, b * half : (b + 1) * half]
            sin_part = total_ref[1, at, b * half : (b + 1) * half]
            swapped = jnp.concatenate([sin_part[rows:], -sin_part[:rows]], axis=0)
            low = lax.dot_general(
                turned, (cos_part - swapped).astype(BF16), nt, preferred_element_type=F32
            ).astype(BF16)
            high = lax.dot_general(
                straight, (cos_part + swapped).astype(BF16), nt, preferred_element_type=F32
            ).astype(BF16)
            if owners:
                each = half // vloc
                for d in range(each):
                    own = slice(d * vloc, (d + 1) * vloc)
                    y_ref[d, b, p * vloc : (p + 1) * vloc, :] = low[own]
                    y_ref[each + d, b, p * vloc : (p + 1) * vloc, :] = high[own]
            else:
                y_ref[b, p, :half, :] = low
                y_ref[b, p, half:, :] = high


def field_kernel(
    dims, pos_ref, box_ref, freq_ref, amp_ref, coeffs_ref, boxes_ref,
    amplitude_ref, amplitude_far_ref, map_ref, map_far_ref,
    x_ref, tile_ref, shift_ref, across_ref, index_ref, y_ref, *rest
):
    dims, pairs = dims
    (
        seg_ref, tables, bases, slot_tables, waves, cos_ref, sin_ref, even_ref, odd_ref, total_ref, slot_map,
    ) = rest
    rows, cols, block, bands, half, band_total, total_rows, per_row, vloc, owners = dims
    step = pl.program_id(0)
    row0 = pos_ref[0] * rows
    chunks = block // LANES
    maps = (map_ref, map_far_ref)
    amplitudes = (amplitude_ref, amplitude_far_ref)

    @pl.when(step == 0)
    def _():
        load_segments(coeffs_ref, boxes_ref, seg_ref)
        width = seg_ref.shape[1]
        groups = rows // 8
        values = [[jnp.zeros((8, LANES), F32)] * 3 for _ in range(groups)]
        base = [jnp.zeros((8, LANES), jnp.int32)] * groups
        for t, piece in tile_row_pieces(seg_ref, per_row, width):
            part = [jnp.broadcast_to(piece[k : k + 1], (8, LANES)) for k in range(7)]
            low, high = part[3][:, :1], part[4][:, :1]
            mid_row = 0.5 * (part[3] + part[4])
            inv_row = 1.0 / (part[4] - part[3] + 1.0)
            mid = 0.5 * (part[5] + part[6])
            inv = 2.0 / (part[6] - part[5] + 1.0)
            slope = 0.5 * part[1] * inv
            slot_tables[0, t : t + 1] = mid[:1]
            slot_tables[1, t : t + 1] = inv[:1]
            for g in range(groups):
                here = (row0 + g * 8 + iota((8, LANES), 0)).astype(F32)
                mine = (here >= low) & (here <= high)
                new = (0.5 * part[0] + part[2] * ((here - mid_row) * inv_row), slope, mid)
                values[g] = [jnp.where(mine, n, v) for n, v in zip(new, values[g])]
                base[g] = jnp.where(mine, t * per_row, base[g])
        for g in range(groups):
            for k in range(3):
                tables[k, g * 8 : (g + 1) * 8] = values[g][k]
            bases[g * 8 : (g + 1) * 8] = base[g]
        for j in range(pairs):
            probe_setup(pos_ref, freq_ref, amp_ref, j, rows, cols, total_rows, waves)
        column_tables(pos_ref[1] * bands, bands, half, band_total, cols, tile_ref, shift_ref)
        total_ref[...] = jnp.zeros_like(total_ref)

    for t in range(SROWS):
        first = jnp.clip(box_ref[0, t * per_row] - row0, 0, rows - 1)
        for side in range(2):
            slot_map[side, t : t + 1, :] = maps[side][pl.ds(first, 1), :] - t * per_row

    column = column_wave(freq_ref, pairs, step, block, cols)
    write_table(cos_ref, sin_ref, tile_ref, shift_ref, step * chunks, chunks)

    for i in range(chunks):
        lanes = slice(i * LANES, (i + 1) * LANES)
        far_lanes = slice((chunks - 1 - i) * LANES, (chunks - i) * LANES)
        near_column = (iota((8, LANES), 1) + (step * block + i * LANES)).astype(F32)
        columns = (near_column, (cols - 1.0) - near_column)
        for side in range(2):
            for t in range(0, SROWS, 8):
                index = slot_map[side, t : t + 8, far_lanes if side else lanes] & (LANES - 1)
                if side:
                    index = reverse(index)
                mid = gather_lanes(slot_tables[0, t : t + 8], index)
                inv = gather_lanes(slot_tables[1, t : t + 8], index)
                across_ref[side, t : t + 8, lanes] = (columns[side] - mid) * inv
                index_ref[side, t : t + 8, lanes] = index
        for g in range(0, rows, 16):
            here = slice(g, g + 16)
            fields = []
            for side in range(2):
                source = far_lanes if side else lanes
                size = amplitudes[side][here, source].astype(F32)
                halves = []
                for h in (0, 8):
                    own = slice(g + h, g + h + 8)
                    index = maps[side][own, source] - bases[own]
                    if side:
                        index = reverse(index)
                    half_phase = gather_lanes(tables[0, own], index) + gather_lanes(
                        tables[1, own], index
                    ) * (columns[side] - gather_lanes(tables[2, own], index))
                    square = half_phase * half_phase
                    s = half_phase * series(SIN_HALF, square)
                    c = series(COS_HALF, square)
                    twice = s + s
                    own_size = size[h : h + 8]
                    if side:
                        own_size = reverse(own_size)
                    halves.append((own_size * (1.0 - twice * s), own_size * (twice * c)))
                both = [
                    jnp.concatenate([halves[0][o], halves[1][o]], axis=0).astype(BF16)
                    for o in range(2)
                ]
                fields.append(both)
            for j in range(pairs):
                emit_pair(
                    j, column, waves, fields, here, lanes, g, rows, x_ref, even_ref, odd_ref
                )

    total_ref[0] += jnp.dot(even_ref[...], cos_ref[...], preferred_element_type=F32)
    total_ref[1] += jnp.dot(odd_ref[...], sin_ref[...], preferred_element_type=F32)

    @pl.when(step == pl.num_programs(0) - 1)
    def _():
        emit_half_way(pairs, total_ref, y_ref, rows, bands, half, vloc, owners)


def row_table_kernel(dims, pos_ref, table_ref):
    rows, cols, bands, focal, band_total, total_rows, sources = dims
    r2 = 2 * rows
    for b in range(bands):
        band = jnp.full((rows, focal), 1, jnp.int32) * (pos_ref[1] * bands + b)
        q = (iota((rows, focal), 1).astype(F32) + (0.5 - focal / 2)) * SAMPLING
        q = focal_scale(q, band, band_total)
        tile_c, tile_s = turn_cos_sin(q * (iota(q.shape, 0).astype(F32) / cols))
        first = iota((sources, focal), 0).astype(F32) * rows + 0.5
        y = first / cols - total_rows / (2.0 * cols)
        shift_c, shift_s = turn_cos_sin(jnp.broadcast_to(q[:1], y.shape) * y)
        for d in range(sources):
            sc, ss = shift_c[d : d + 1], shift_s[d : d + 1]
            c = (tile_c * sc - tile_s * ss).astype(BF16)
            s_value = tile_s * sc + tile_c * ss
            s = s_value.astype(BF16)
            table_ref[b, d * r2 : d * r2 + rows, :focal] = c
            table_ref[b, d * r2 : d * r2 + rows, focal:] = (-s_value).astype(BF16)
            table_ref[b, d * r2 + rows : (d + 1) * r2, :focal] = s
            table_ref[b, d * r2 + rows : (d + 1) * r2, focal:] = c


def focal_kernel(dims, y_ref, target_ref, table_ref, h_ref):
    rows, sources, scale = dims
    r2 = 2 * rows
    lhs = jnp.concatenate([y_ref[d] for d in range(sources)], axis=1)
    f = jnp.dot(lhs, table_ref[...], preferred_element_type=F32)
    residual = (f * (2.0 * scale) - target_ref[...]).astype(BF16)
    spread = lax.dot_general(
        residual, table_ref[...], (((1,), (1,)), ((), ())), preferred_element_type=F32
    )
    for d in range(sources):
        h_ref[d] = spread[:, d * r2 : (d + 1) * r2].astype(BF16)


def fold_hidden(pairs, h_ref, left_ref, rows, bands, half, vloc, sources):
    r2 = 2 * rows
    nt = (((1,), (1,)), ((), ()))
    m = iota((half, 2 * half), 0)
    v = iota((half, 2 * half), 1)
    upper = (v == half + m).astype(F32)
    lower = (v == half - 1 - m).astype(F32)
    even, odd = (upper + lower).astype(BF16), (upper - lower).astype(BF16)
    same = (iota((r2, r2), 0) == iota((r2, r2), 1)).astype(F32).astype(BF16)
    for b in range(bands):
        for p in range(2 * pairs):
            if sources:
                block_h = jnp.concatenate(
                    [h_ref[d, b, p * vloc : (p + 1) * vloc, :] for d in range(sources)], axis=0
                )
            else:
                block_h = h_ref[b, p]

            def fold(mirror):
                folded = jnp.dot(mirror, block_h, preferred_element_type=F32).astype(BF16)
                return lax.dot_general(same, folded, nt, preferred_element_type=F32)

            plus, minus = fold(even), fold(odd)
            at = slice(p * r2, (p + 1) * r2)
            left_ref[0, at, b * half : (b + 1) * half] = plus.astype(BF16)
            left_ref[1, at, b * half : (b + 1) * half] = jnp.concatenate(
                [-minus[rows:], minus[:rows]], axis=0
            ).astype(BF16)


def weight_kernel(
    dims, pos_ref, box_ref, h_ref, x_ref, tile_ref, shift_ref, across_ref, index_ref,
    out_ref, left_ref, pick_ref, cos_ref, sin_ref, p_ref, q_ref, weight_ref, sums_ref, term_ref,
):
    rows, cols, block, part, bands, half, per_row, pairs, vloc, sources, scale = dims
    step = pl.program_id(0)
    row0 = pos_ref[0] * rows
    r2 = 2 * rows
    nt = (((1,), (1,)), ((), ()))

    @pl.when(step == 0)
    def _():
        fold_hidden(pairs, h_ref, left_ref, rows, bands, half, vloc, sources)
        slot = iota((SROWS, r2), 0)
        lane = iota((SROWS, r2), 1)
        here = (row0 + lane % rows).astype(F32)
        low = jnp.zeros((SROWS, r2), F32)
        high = jnp.zeros((SROWS, r2), F32)
        for t in range(SROWS):
            low = jnp.where(slot == t, box_ref[0, t * per_row].astype(F32), low)
            high = jnp.where(slot == t, box_ref[1, t * per_row].astype(F32), high)
        mine = ((here >= low) & (here <= high)).astype(F32)
        down = mine * ((here - 0.5 * (low + high)) / (0.5 * (high - low + 1.0)))
        down_high = down.astype(BF16)
        pick_ref[:SROWS] = mine.astype(BF16)
        pick_ref[SROWS : 2 * SROWS] = down_high
        pick_ref[2 * SROWS :] = (down - down_high.astype(F32)).astype(BF16)
        out_ref[...] = jnp.zeros_like(out_ref)

    tiles = part // LANES
    for k in range(block // part):
        slot = k % 2
        write_table(
            cos_ref.at[slot], sin_ref.at[slot], tile_ref, shift_ref,
            step * (block // LANES) + k * tiles, tiles,
        )
        p_ref[slot] = lax.dot_general(left_ref[0], cos_ref[slot], nt, preferred_element_type=F32)
        q_ref[slot] = lax.dot_general(left_ref[1], sin_ref[slot], nt, preferred_element_type=F32)
        for i in range(tiles):
            lanes = slice(i * LANES, (i + 1) * LANES)
            at = slice(k * part + i * LANES, k * part + (i + 1) * LANES)
            for g in range(0, rows, 16):
                near, far = None, None
                for p in range(2 * pairs):
                    j, first = divmod(p, 2)
                    re = slice(p * r2 + g, p * r2 + g + 16)
                    im = slice(p * r2 + rows + g, p * r2 + rows + g + 16)
                    xre = slice(first * r2 + g, first * r2 + g + 16)
                    xim = slice(first * r2 + rows + g, first * r2 + rows + g + 16)
                    p_re, p_im = p_ref[slot, re, lanes], p_ref[slot, im, lanes]
                    q_re, q_im = q_ref[slot, re, lanes], q_ref[slot, im, lanes]
                    x = [
                        [x_ref[j, side, rows_, at].astype(F32) for rows_ in (xre, xim)]
                        for side in range(2)
                    ]
                    near_term = x[0][0] * (p_im + q_im) - x[0][1] * (p_re + q_re)
                    far_term = x[1][0] * (p_im - q_im) - x[1][1] * (p_re - q_re)
                    near = near_term if near is None else near + near_term
                    far = far_term if far is None else far + far_term
                for side, value in enumerate((near, far)):
                    high = value.astype(BF16)
                    to = slice(side * block + at.start, side * block + at.stop)
                    weight_ref[g : g + 16, to] = high
                    weight_ref[rows + g : rows + g + 16, to] = (
                        value - high.astype(F32)
                    ).astype(BF16)
    sums = jnp.dot(pick_ref[...], weight_ref[...], preferred_element_type=F32)
    for side in range(2):
        mine = sums[:, side * block : (side + 1) * block]
        sums_ref[step, side, 0] = mine[:SROWS]
        sums_ref[step, side, 1] = mine[:SROWS] * across_ref[side]
        sums_ref[step, side, 2] = mine[SROWS : 2 * SROWS] + mine[2 * SROWS :]
        term_ref[step, side] = index_ref[side]

    @pl.when(step == pl.num_programs(0) - 1)
    def _():
        tops = [box_ref[0, t * per_row] for t in range(SROWS)]
        bottoms = [box_ref[1, t * per_row] for t in range(SROWS)]
        first = sum((bottom < row0).astype(jnp.int32) for bottom in bottoms)
        last = sum((top < row0 + rows).astype(jnp.int32) for top in tops)

        def tile_row(t, carry):
            def add(i, total):
                for side in range(2):
                    index = term_ref[i, side, pl.ds(t, 1), :]
                    inside = (iota((LANES, block), 0) == index).astype(F32).astype(BF16)
                    terms = [sums_ref[i, side, q, pl.ds(t, 1), :] for q in range(3)]
                    highs = [x.astype(BF16).astype(F32) for x in terms]
                    lows = [x - h for x, h in zip(terms, highs)]
                    stacked = jnp.concatenate(highs + lows + lows[:2], axis=0).astype(BF16)
                    total = total + lax.dot_general(
                        stacked, inside, nt, preferred_element_type=F32
                    )
                return total

            total = lax.fori_loop(0, pl.num_programs(0), add, jnp.zeros((8, LANES), F32))
            for q in range(3):
                out_ref[q, pl.ds(t, 1)] = (total[q : q + 1] + total[q + 3 : q + 4]) * scale
            return carry

        lax.fori_loop(first, last, tile_row, 0)


def body(amplitude, seg_map, seg_box, seg_coeffs, probe_freq, probe_amp, measured):
    rows, cols = amplitude.shape
    owners = lax.axis_size("row")
    band_axis = lax.axis_size("band")
    total_rows = rows * owners
    bands, vloc, probes, _, focal = measured.shape
    pairs = probes // 2
    half = focal // 2
    band_total = bands * band_axis
    segments = seg_coeffs.shape[1]
    per_row = segments // SROWS
    r2 = 2 * rows
    normf = 1.0 / math.sqrt(total_rows * cols)
    aligned = vloc % 16 == 0
    half_cols = cols // 2
    field_block, block, part = BLOCKS
    k_width = bands * half

    pos = jnp.stack([lax.axis_index("row"), lax.axis_index("band")]).astype(jnp.int32)
    width = -(-(segments + LANES) // LANES) * LANES
    smem = pl.BlockSpec(memory_space=pltpu.SMEM)
    whole = pl.BlockSpec(memory_space=pltpu.VMEM)
    params = pltpu.CompilerParams(dimension_semantics=("arbitrary",))

    def resident(shape):
        return pl.BlockSpec(shape, lambda i: (0,) * len(shape), pipeline_mode=pl.Buffered(1))

    def cost(flops, moved):
        return pl.CostEstimate(flops=int(flops), bytes_accessed=int(moved), transcendentals=0)

    def slot_spec(block):
        return pl.BlockSpec((2, SROWS, block), lambda i: (0, 0, i))

    near = pl.BlockSpec((rows, field_block), lambda i: (0, i))
    far = pl.BlockSpec((rows, field_block), lambda i: (0, cols // field_block - 1 - i))
    tile_shape = (2, LANES, k_width)
    shift_shape = (2, half_cols // LANES, k_width)
    arrays = 2 * pairs
    y_dims = (owners, bands, arrays * vloc, r2) if aligned else (bands, arrays, focal, r2)
    y_spec = pl.BlockSpec(y_dims, lambda i: (0,) * len(y_dims))
    y_shape = jax.ShapeDtypeStruct(y_dims, BF16)
    def field_dims(block):
        return (
            rows, cols, block, bands, half, band_total, total_rows, per_row, vloc, aligned
        )

    matmul = 2 * 4 * rows * half_cols * k_width * 2

    def table_scratch(block):
        return [pltpu.VMEM((block, k_width), BF16), pltpu.VMEM((block, k_width), BF16)]

    fields, tile, shift, across, index, half_way = pl.pallas_call(
        functools.partial(field_kernel, (field_dims(field_block), pairs)),
        grid=(half_cols // field_block,),
        in_specs=[
            smem, smem, smem, smem,
            resident(seg_coeffs.shape),
            resident(seg_box.shape),
            near, far, near, far,
        ],
        out_specs=[
            pl.BlockSpec((pairs, 2, 4 * rows, field_block), lambda i: (0, 0, 0, i)),
            pl.BlockSpec(tile_shape, lambda i: (0, 0, 0)),
            pl.BlockSpec(shift_shape, lambda i: (0, 0, 0)),
            slot_spec(field_block),
            slot_spec(field_block),
            y_spec,
        ],
        out_shape=[
            jax.ShapeDtypeStruct((pairs, 2, 4 * rows, half_cols), BF16),
            jax.ShapeDtypeStruct(tile_shape, F32),
            jax.ShapeDtypeStruct(shift_shape, F32),
            jax.ShapeDtypeStruct((2, SROWS, half_cols), F32),
            jax.ShapeDtypeStruct((2, SROWS, half_cols), jnp.int32),
            y_shape,
        ],
        scratch_shapes=[
            pltpu.VMEM((8, width), F32),
            pltpu.VMEM((3, rows, LANES), F32),
            pltpu.VMEM((rows, LANES), jnp.int32),
            pltpu.VMEM((2, SROWS, LANES), F32),
            pltpu.VMEM((2 * pairs, rows, LANES), F32),
            *table_scratch(field_block),
            pltpu.VMEM((4 * pairs * rows, field_block), BF16),
            pltpu.VMEM((4 * pairs * rows, field_block), BF16),
            pltpu.VMEM((2, 4 * pairs * rows, k_width), F32),
            pltpu.VMEM((2, SROWS, field_block), jnp.int32),
        ],
        compiler_params=params,
        cost_estimate=cost(4 * matmul, 20e6),
        name="field",
    )(pos, seg_box, probe_freq, probe_amp, seg_coeffs, seg_box,
      amplitude, amplitude, seg_map, seg_map)

    if not aligned:
        half_way = (
            half_way.reshape(bands, arrays, owners, vloc, r2)
            .transpose(2, 0, 1, 3, 4)
            .reshape(owners, bands, arrays * vloc, r2)
        )
    received = lax.all_to_all(half_way, "row", split_axis=0, concat_axis=0, tiled=True)

    row_table = pl.pallas_call(
        functools.partial(
            row_table_kernel, (rows, cols, bands, focal, band_total, total_rows, owners)
        ),
        in_specs=[smem],
        out_specs=whole,
        out_shape=jax.ShapeDtypeStruct((bands, owners * r2, 2 * focal), BF16),
        cost_estimate=cost(1e6, 2e6),
        name="row_table",
    )(pos)

    plus, minus = measured[:, :, 0::2], measured[:, :, 1::2]
    total, difference = plus + minus, plus - minus
    turned = jnp.stack([difference[:, :, :, 1], -difference[:, :, :, 0]], axis=3)
    targets = jnp.stack([total, turned], axis=3)
    targets = targets.transpose(0, 2, 3, 1, 4, 5).reshape(bands, arrays * vloc, 2 * focal)

    y_block = pl.BlockSpec((owners, None, arrays * vloc, r2), lambda b: (0, b, 0, 0))
    spread = pl.pallas_call(
        functools.partial(focal_kernel, (rows, owners, normf)),
        grid=(bands,),
        in_specs=[
            y_block,
            pl.BlockSpec((None, arrays * vloc, 2 * focal), lambda b: (b, 0, 0)),
            pl.BlockSpec((None, owners * r2, 2 * focal), lambda b: (b, 0, 0)),
        ],
        out_specs=y_block,
        out_shape=jax.ShapeDtypeStruct((owners, bands, arrays * vloc, r2), BF16),
        compiler_params=params,
        cost_estimate=cost(8 * bands * arrays * vloc * owners * r2 * focal, 4e6),
        name="focal",
    )(received, targets, row_table)
    hidden = lax.all_to_all(spread, "row", split_axis=0, concat_axis=0, tiled=True)
    if not aligned:
        hidden = (
            hidden.reshape(owners, bands, arrays, vloc, r2)
            .transpose(1, 2, 0, 3, 4)
            .reshape(bands, arrays, focal, r2)
        )

    scale = 2.0 * normf / (band_total * probes)
    steps = half_cols // block
    weight_dims = (
        rows, cols, block, part, bands, half, per_row, pairs, vloc,
        owners if aligned else 0, scale,
    )
    local = pl.pallas_call(
        functools.partial(weight_kernel, weight_dims),
        grid=(steps,),
        in_specs=[
            smem, smem, resident(hidden.shape),
            pl.BlockSpec((pairs, 2, 4 * rows, block), lambda i: (0, 0, 0, i)),
            resident(tile_shape), resident(shift_shape), slot_spec(block), slot_spec(block),
        ],
        out_specs=pl.BlockSpec((3, SROWS, LANES), lambda i: (0, 0, 0)),
        out_shape=jax.ShapeDtypeStruct((3, SROWS, LANES), F32),
        scratch_shapes=[
            pltpu.VMEM((2, 4 * pairs * rows, k_width), BF16),
            pltpu.VMEM((3 * SROWS, r2), BF16),
            pltpu.VMEM((2, part, k_width), BF16),
            pltpu.VMEM((2, part, k_width), BF16),
            pltpu.VMEM((2, 4 * pairs * rows, part), F32),
            pltpu.VMEM((2, 4 * pairs * rows, part), F32),
            pltpu.VMEM((r2, 2 * block), BF16),
            pltpu.VMEM((steps, 2, 3, SROWS, block), F32),
            pltpu.VMEM((steps, 2, SROWS, block), jnp.int32),
        ],
        compiler_params=params,
        cost_estimate=cost(4 * matmul, 20e6),
        name="weight",
    )(pos, seg_box, hidden, fields, tile, shift, across, index)

    devices = owners * band_axis
    axes = ("band", "row")
    shares = local.reshape(devices, -1)
    mine = jnp.sum(lax.all_to_all(shares, axes, split_axis=0, concat_axis=0, tiled=True), axis=0)
    copies = jnp.broadcast_to(mine[None], shares.shape)
    gathered = lax.all_to_all(copies, axes, split_axis=0, concat_axis=0, tiled=True)
    return gathered.reshape(3, SROWS, LANES)[:, :, :per_row].reshape(3, segments)


def solution(mesh):
    in_specs = (
        P("row", None),
        P("row", None),
        P(),
        P(),
        P(),
        P(),
        P("band", "row", None, None, None),
    )
    return jax.shard_map(body, mesh=mesh, in_specs=in_specs, out_specs=P(), check_vma=False)
```

time: 105 us -> 97.8 us (0.931)
  Pallas kernels: 40.4 us -> 35.2 us
  waiting for transfers between devices: 12 us -> 10.4 us
    pallas_call x3 -> x4, Pallas kernels: 40.4 us -> 35.2 us  [the longest x1 17.2 us: body(): pl.pallas_call(functools.partial(field_kernel, (field_dims(field_block),...]
    all_to_all x1, waiting for transfers between devices: 12 us -> 10.4 us  [body(): lax.all_to_all(half_way, 'row', split_axis=0, concat_axis=0, tiled=True)]
  transfers between devices with their start and end apart: 1 -> 1, of which waited for: 1 -> 1; matrix products, arithmetic and copies ran while one was open for 3% -> 2% of each run, Pallas kernels for 0% -> 3%
where the time goes in v2:
time: 97.8 us; the launch traced here: 97.4 us
  blocking collectives  39.9 us (41%)
  Pallas kernels  35.2 us (36%)
  waiting for transfers between devices  10.4 us (11%)
  starting transfers between devices  6.35 us (6%)
  local copies, waits for them, and re-layouts  3.87 us (4%)
  other arithmetic  1.6 us (2%)
    all_to_all x1, blocking collectives, body(): lax.all_to_all(spread, 'row', split_axis=0, concat_axis=0, tiled=True)  19.5 us
    pallas_call x1, Pallas kernels, body(): pl.pallas_call(functools.partial(field_kernel, (field_dims(field_block),...  17.2 us
    pallas_call x1, Pallas kernels, body(): pl.pallas_call(functools.partial(weight_kernel, weight_dims), grid=(steps...  11.9 us
    all_to_all x1, blocking collectives, body(): lax.all_to_all(shares, axes, split_axis=0, concat_axis=0, tiled=True)  11.5 us
    all_to_all x1, waiting for transfers between devices, body(): lax.all_to_all(half_way, 'row', split_axis=0, concat_axis=0, tiled=True)  10.4 us
    all_to_all x1, blocking collectives, body(): lax.all_to_all(copies, axes, split_axis=0, concat_axis=0, tiled=True)  8.94 us
    all_to_all x1, starting transfers between devices, body(): lax.all_to_all(half_way, 'row', split_axis=0, concat_axis=0, tiled=True)  6.35 us
    pallas_call x1, Pallas kernels, body(): pl.pallas_call(functools.partial(focal_kernel, (rows, owners, normf)), gr...  3.52 us
  transfers between devices with their start and end apart: 1, of which 1 were waited for; matrix products, arithmetic and copies ran while one was open for 2% of the time, Pallas kernels for 3%

profile of v2, /device:TPU:0, one launch (start us, length us, event | category | flops | bytes accessed | tf_op | source)
XLA Modules:
  0.0 97.4 jit_solution(2480500552164948715)
XLA Ops:
  0.0 0.6 pad_add_fusion.pos_ref
  0.6 0.0 copy-start.1
  0.6 17.2 %field.1 = (bf16[2,2,256,4096]{3,2,1,0:T(8,128)(2,1)}, f32[2,128,256]{2,1,0:T(8,128)}, f32[2,32,256]{2,1,0:T(8,128)}, f32[2,16,4096]{2,1,0:T(8,128)}, s32[2,16,4...) custom-call(s32[2]{0:T(128)} %pad_add_fusion.pos_ref, s32[4,1200]{1,0:T(4,128)} %box_ref.3, s32[2,2]{1,0:T(2,128)} %freq_ref.1, ...), custom_call_target="tpu_custom_call" | custom-call | flops 4294967296 | bytes 20000000 | tf_op jit(solution)/shard_map/field/pallas_call | solution.py:513
  17.8 6.4 %all-to-all-start = ((bf16[8,2,128,128]{3,2,1,0:T(8,128)(2,1)}), bf16[8,2,128,128]{3,2,1,0:T(8,128)(2,1)S(1)}, u32[]{:S(2)}, u32[]{:S(2)}) async-start(bf16[8,2,128,128]{3,2,1,0:T(8,128)(2,1)} %get-tuple-element.11), calls=%async_computation | async-start | bytes 1048576 | tf_op jit(solution)/shard_map/all_to_all | solution.py:562
  24.2 0.0 copy-done.1
  24.2 0.2 add_bitcast_fusion
  24.4 0.2 fusion
  24.6 0.2 maximum_bitcast_fusion.1
  24.8 0.2 maximum_bitcast_fusion
  25.1 0.2 copy.9
  25.3 1.2 %reshape.20.target_ref = f32[2,128,512]{2,1,0:T(8,128)} reshape(f32[2,2,2,32,2,256]{5,4,3,2,1,0:T(2,128)S(1)} %copy.9) | data formatting | bytes 1048576 | tf_op jit(solution)/shard_map/reshape | solution.py:579
  26.5 2.6 %row_table.1.table_ref = bf16[2,1024,512]{2,1,0:T(8,128)(2,1)} custom-call(s32[2]{0:T(128)} %pad_add_fusion.pos_ref), custom_call_target="tpu_custom_call" | custom-call | flops 1000000 | bytes 2000000 | tf_op jit(solution)/shard_map/row_table/pallas_call | solution.py:564
  29.1 10.4 %all-to-all-done.y_ref = bf16[8,2,128,128]{3,2,1,0:T(8,128)(2,1)S(1)} async-done(((bf16[8,2,128,128]{3,2,1,0:T(8,128)(2,1)}), bf16[8,2,128,128]{3,2,1,0:T(8,128)(2,1)S(1)}, u32[]{:S(2)}, u32[]{:S(2)}) %all-to-all-start) | async-done | bytes 524320 | tf_op jit(solution)/shard_map/all_to_all | solution.py:562
  39.5 0.0 copy-start
  39.5 0.8 copy-done
  40.3 3.5 %focal.1 = bf16[8,2,128,128]{3,2,1,0:T(8,128)(2,1)} custom-call(bf16[8,2,128,128]{3,2,1,0:T(8,128)(2,1)} %copy-done, f32[2,128,512]{2,1,0:T(8,128)} %reshape.20.target_ref, bf16[2,1024,512]{2,1,0:T(8,128)(2,1)} %row_table.1.table_ref), custom_call_target="tpu_custom_call" | custom-call | flops 536870912 | bytes 4000000 | tf_op jit(solution)/shard_map/focal/pallas_call | solution.py:582
  43.8 19.5 %all_to_all.26.h_ref = bf16[8,2,128,128]{3,2,1,0:T(8,128)(2,1)} all-to-all(bf16[8,2,128,128]{3,2,1,0:T(8,128)(2,1)} %focal.1), channel_id=1, replica_groups=mesh['band'=4,'row'=8] {'row'}, dimensions={0} | all-to-all | bytes 1048576 | tf_op jit(solution)/shard_map/all_to_all | solution.py:596
  63.3 11.9 %weight.1 = f32[3,16,128]{2,1,0:T(8,128)} custom-call(s32[2]{0:T(128)} %pad_add_fusion.pos_ref, s32[4,1200]{1,0:T(4,128)} %box_ref.3, bf16[8,2,128,128]{3,2,1,0:T(8,128)(2,1)} %all_to_all.26.h_ref, bf16[2,2,256,4096]{3,2,1,0:T(8,128)(2,1)} %get-tuple-element.12.x_ref, f32[2,128,256]{2,1,0:T(8,128)} %get-tuple-element.13.tile_ref, ...), custom_call_target="tpu_custom_call" | custom-call | flops 4294967296 | bytes 20000000 | tf_op jit(solution)/shard_map/weight/pallas_call | solution.py:610
  75.2 0.8 all_to_all.21
  76.0 11.5 %all_to_all.27 = f32[32,1,192]{2,1,0:T(1,128)S(1)} all-to-all(f32[32,1,192]{2,1,0:T(1,128)S(1)} %all_to_all.21), channel_id=1, replica_groups=mesh['band'=4,'row'=8] {'band','row'}, dimensions={0} | all-to-all | bytes 49152 | tf_op jit(solution)/shard_map/all_to_all | solution.py:639
  87.5 0.1 reduce_sum.9
  87.6 8.9 %all_to_all.28 = f32[32,1,192]{2,1,0:T(1,128)S(1)} all-to-all(f32[32,1,192]{2,1,0:T(1,128)S(1)} %broadcast_in_dim.2), channel_id=1, replica_groups=mesh['band'=4,'row'=8] {'band','row'}, dimensions={0} | all-to-all | bytes 49152 | tf_op jit(solution)/shard_map/all_to_all | solution.py:641
  96.5 0.1 reduce.1
  96.6 0.1 reshape.21
  96.7 0.7 reshape.22
  (1 shorter events, 0.0 us)
Async XLA Ops:
  0.6 23.6 %copy-start.1 = (f32[2,32,4,2,256]{4,3,2,1,0:T(2,128)S(1)}, f32[2,32,4,2,256]{4,3,2,1,0:T(2,128)}, u32[]{:S(2)}) copy-start(f32[2,32,4,2,256]{4,3,2,1,0:T(2,128)} %param.13) | copy-start | bytes 1572868
  17.8 21.7 %all-to-all-start = ((bf16[8,2,128,128]{3,2,1,0:T(8,128)(2,1)}), bf16[8,2,128,128]{3,2,1,0:T(8,128)(2,1)S(1)}, u32[]{:S(2)}, u32[]{:S(2)}) async-start(bf16[8,2,128,128]{3,2,1,0:T(8,128)(2,1)} %get-tuple-element.11), calls=%async_computation | async-start | bytes 1048576 | tf_op jit(solution)/shard_map/all_to_all | solution.py:562
  39.5 0.8 copy-start

commit v3 on v2

--- a/solution.py
+++ b/solution.py
@@ -358,7 +358,8 @@
 
 def weight_kernel(
     dims, pos_ref, box_ref, h_ref, x_ref, tile_ref, shift_ref, across_ref, index_ref,
-    out_ref, left_ref, pick_ref, cos_ref, sin_ref, p_ref, q_ref, weight_ref, sums_ref, term_ref,
+    out_ref, give_ref, left_ref, pick_ref, cos_ref, sin_ref, p_ref, q_ref, weight_ref, sums_ref,
+    term_ref, flat_ref,
 ):
     rows, cols, block, part, bands, half, per_row, pairs, vloc, sources, scale = dims
     step = pl.program_id(0)
@@ -383,7 +384,6 @@
         pick_ref[:SROWS] = mine.astype(BF16)
         pick_ref[SROWS : 2 * SROWS] = down_high
         pick_ref[2 * SROWS :] = (down - down_high.astype(F32)).astype(BF16)
-        out_ref[...] = jnp.zeros_like(out_ref)
 
     tiles = part // LANES
     for k in range(block // part):
@@ -440,8 +440,8 @@
         def tile_row(t, carry):
             def add(i, total):
                 for side in range(2):
-                    index = term_ref[i, side, pl.ds(t, 1), :]
-                    inside = (iota((LANES, block), 0) == index).astype(F32).astype(BF16)
+                    index = term_ref[i, side, pl.ds(t, 1), :].astype(F32).astype(BF16)
+                    inside = jnp.where(tile_index == index, one, zero)
                     terms = [sums_ref[i, side, q, pl.ds(t, 1), :] for q in range(3)]
                     highs = [x.astype(BF16).astype(F32) for x in terms]
                     lows = [x - h for x, h in zip(terms, highs)]
@@ -452,11 +452,27 @@
                 return total
 
             total = lax.fori_loop(0, pl.num_programs(0), add, jnp.zeros((8, LANES), F32))
-            for q in range(3):
-                out_ref[q, pl.ds(t, 1)] = (total[q : q + 1] + total[q + 3 : q + 4]) * scale
+            total = jnp.where(iota((8, LANES), 1) < per_row, total, 0.0)
+            padding = jnp.zeros((8, flat_ref.shape[1] - LANES), F32)
+            wide = jnp.concatenate([total, padding], axis=1)
+            flat_ref[...] += pltpu.roll(wide, t * per_row, axis=1)
             return carry
 
+        tile_index = iota((LANES, block), 0).astype(F32).astype(BF16)
+        one = jnp.ones((LANES, block), BF16)
+        zero = jnp.zeros((LANES, block), BF16)
+        flat_ref[...] = jnp.zeros_like(flat_ref)
         lax.fori_loop(first, last, tile_row, 0)
+        odd = pos_ref[0] % 2 == 1
+        pieces = flat_ref.shape[1] // (2 * LANES)
+        for q in range(3):
+            value = (flat_ref[q : q + 1] + flat_ref[q + 3 : q + 4]) * scale
+            for i in range(pieces):
+                low = value[:, i * LANES : (i + 1) * LANES]
+                high = value[:, (pieces + i) * LANES : (pieces + i + 1) * LANES]
+                at = q * pieces + i
+                out_ref[at : at + 1] = jnp.where(odd, high, low)
+                give_ref[at : at + 1] = jnp.where(odd, low, high)
 
 
 def body(amplitude, seg_map, seg_box, seg_coeffs, probe_freq, probe_amp, measured):
@@ -607,7 +623,9 @@
         rows, cols, block, part, bands, half, per_row, pairs, vloc,
         owners if aligned else 0, scale,
     )
-    local = pl.pallas_call(
+    pieces = -(-segments // (2 * LANES))
+    share = jax.ShapeDtypeStruct((3 * pieces, LANES), F32)
+    kept, given = pl.pallas_call(
         functools.partial(weight_kernel, weight_dims),
         grid=(steps,),
         in_specs=[
@@ -615,8 +633,8 @@
             pl.BlockSpec((pairs, 2, 4 * rows, block), lambda i: (0, 0, 0, i)),
             resident(tile_shape), resident(shift_shape), slot_spec(block), slot_spec(block),
         ],
-        out_specs=pl.BlockSpec((3, SROWS, LANES), lambda i: (0, 0, 0)),
-        out_shape=jax.ShapeDtypeStruct((3, SROWS, LANES), F32),
+        out_specs=[pl.BlockSpec(share.shape, lambda i: (0, 0))] * 2,
+        out_shape=[share, share],
         scratch_shapes=[
             pltpu.VMEM((2, 4 * pairs * rows, k_width), BF16),
             pltpu.VMEM((3 * SROWS, r2), BF16),
@@ -627,19 +645,31 @@
             pltpu.VMEM((r2, 2 * block), BF16),
             pltpu.VMEM((steps, 2, 3, SROWS, block), F32),
             pltpu.VMEM((steps, 2, SROWS, block), jnp.int32),
+            pltpu.VMEM((8, 2 * pieces * LANES), F32),
         ],
         compiler_params=params,
         cost_estimate=cost(4 * matmul, 20e6),
         name="weight",
     )(pos, seg_box, hidden, fields, tile, shift, across, index)
 
+    axes = ("band", "row")
     devices = owners * band_axis
-    axes = ("band", "row")
-    shares = local.reshape(devices, -1)
-    mine = jnp.sum(lax.all_to_all(shares, axes, split_axis=0, concat_axis=0, tiled=True), axis=0)
-    copies = jnp.broadcast_to(mine[None], shares.shape)
-    gathered = lax.all_to_all(copies, axes, split_axis=0, concat_axis=0, tiled=True)
-    return gathered.reshape(3, SROWS, LANES)[:, :, :per_row].reshape(3, segments)
+    groups = [[d for d in range(devices) if d % 2 == core] for core in range(2)]
+
+    def swap_cores(array):
+        return lax.ppermute(array, "row", [(i, i ^ 1) for i in range(owners)])
+
+    mine = kept + swap_cores(given)
+    copies = jnp.broadcast_to(mine[None], (devices // 2,) + mine.shape)
+    everyones = lax.all_to_all(
+        copies, axes, split_axis=0, concat_axis=0, tiled=True, axis_index_groups=groups
+    )
+    mine = jnp.sum(everyones, axis=0)
+    other = swap_cores(mine)
+    odd = lax.axis_index("row") % 2 == 1
+    halves = [jnp.where(odd, other, mine), jnp.where(odd, mine, other)]
+    halves = [x.reshape(3, pieces * LANES) for x in halves]
+    return jnp.concatenate(halves, axis=1)[:, :segments]
 
 
 def solution(mesh):

time: 97.8 us -> 92.7 us (0.948)
  blocking collectives: 39.9 us -> 33.8 us
  waiting for transfers between devices: 10.4 us -> 12.6 us
  local copies, waits for them, and re-layouts: 3.87 us -> 2.26 us
  other arithmetic: 1.6 us -> 2.8 us
    all_to_all x2 -> x1, blocking collectives: 20.4 us -> 14.3 us  [body(): lax.all_to_all(copies, axes, split_axis=0, concat_axis=0, tiled=True, axi...]
    ppermute x0 -> x2, waiting for transfers between devices: none -> 2.19 us  [swap_cores(): return lax.ppermute(array, 'row', [(i, i ^ 1) for i in range(owners)])]
  transfers between devices with their start and end apart: 1 -> 3, of which waited for: 1 -> 3; matrix products, arithmetic and copies ran while one was open for 2% -> 2% of each run, Pallas kernels for 3% -> 3%
where the time goes in v3:
time: 92.7 us; the launch traced here: 92.8 us
  Pallas kernels  34.5 us (37%)
  blocking collectives  33.8 us (36%)
  waiting for transfers between devices  12.6 us (14%)
  starting transfers between devices  6.8 us (7%)
  other arithmetic  2.8 us (3%)
  local copies, waits for them, and re-layouts  2.26 us (2%)
    all_to_all x1, blocking collectives, body(): lax.all_to_all(spread, 'row', split_axis=0, concat_axis=0, tiled=True)  19.5 us
    pallas_call x1, Pallas kernels, body(): pl.pallas_call(functools.partial(field_kernel, (field_dims(field_block),...  17.2 us
    all_to_all x1, blocking collectives, body(): lax.all_to_all(copies, axes, split_axis=0, concat_axis=0, tiled=True, axi...  14.3 us
    pallas_call x1, Pallas kernels, body(): pl.pallas_call(functools.partial(weight_kernel, weight_dims), grid=(steps...  11.1 us
    all_to_all x1, waiting for transfers between devices, body(): lax.all_to_all(half_way, 'row', split_axis=0, concat_axis=0, tiled=True)  10.4 us
    all_to_all x1, starting transfers between devices, body(): lax.all_to_all(half_way, 'row', split_axis=0, concat_axis=0, tiled=True)  6.36 us
    pallas_call x1, Pallas kernels, body(): pl.pallas_call(functools.partial(focal_kernel, (rows, owners, normf)), gr...  3.53 us
    pallas_call x1, Pallas kernels, body(): pl.pallas_call(functools.partial(row_table_kernel, (rows, cols, bands, fo...  2.58 us
  transfers between devices with their start and end apart: 3, of which 3 were waited for; matrix products, arithmetic and copies ran while one was open for 2% of the time, Pallas kernels for 3%

profile of v3, /device:TPU:0, one launch (start us, length us, event | category | flops | bytes accessed | tf_op | source)
XLA Modules:
  0.0 92.8 jit_solution(5252937213602920295)
XLA Ops:
  0.0 0.6 pad_add_fusion.pos_ref
  0.6 0.0 copy-start.1
  0.6 17.2 %field.1 = (bf16[2,2,256,4096]{3,2,1,0:T(8,128)(2,1)}, f32[2,128,256]{2,1,0:T(8,128)}, f32[2,32,256]{2,1,0:T(8,128)}, f32[2,16,4096]{2,1,0:T(8,128)}, s32[2,16,4...) custom-call(s32[2]{0:T(128)} %pad_add_fusion.pos_ref, s32[4,1200]{1,0:T(4,128)} %box_ref.3, s32[2,2]{1,0:T(2,128)} %freq_ref.1, ...), custom_call_target="tpu_custom_call" | custom-call | flops 4294967296 | bytes 20000000 | tf_op jit(solution)/shard_map/field/pallas_call | solution.py:529
  17.8 6.4 %all-to-all-start = ((bf16[8,2,128,128]{3,2,1,0:T(8,128)(2,1)}), bf16[8,2,128,128]{3,2,1,0:T(8,128)(2,1)S(1)}, u32[]{:S(2)}, u32[]{:S(2)}) async-start(bf16[8,2,128,128]{3,2,1,0:T(8,128)(2,1)} %get-tuple-element.13), calls=%async_computation | async-start | bytes 1048576 | tf_op jit(solution)/shard_map/all_to_all | solution.py:578
  24.2 0.0 copy-done.1
  24.2 0.2 add_bitcast_fusion
  24.4 0.2 fusion
  24.6 0.2 maximum_bitcast_fusion.1
  24.9 0.2 maximum_bitcast_fusion
  25.1 0.2 copy.10
  25.3 1.2 %reshape.10.target_ref = f32[2,128,512]{2,1,0:T(8,128)} reshape(f32[2,2,2,32,2,256]{5,4,3,2,1,0:T(2,128)S(1)} %copy.10) | data formatting | bytes 1048576 | tf_op jit(solution)/shard_map/reshape | solution.py:595
  26.5 2.6 %row_table.1.table_ref = bf16[2,1024,512]{2,1,0:T(8,128)(2,1)} custom-call(s32[2]{0:T(128)} %pad_add_fusion.pos_ref), custom_call_target="tpu_custom_call" | custom-call | flops 1000000 | bytes 2000000 | tf_op jit(solution)/shard_map/row_table/pallas_call | solution.py:580
  29.1 10.4 %all-to-all-done.y_ref = bf16[8,2,128,128]{3,2,1,0:T(8,128)(2,1)S(1)} async-done(((bf16[8,2,128,128]{3,2,1,0:T(8,128)(2,1)}), bf16[8,2,128,128]{3,2,1,0:T(8,128)(2,1)S(1)}, u32[]{:S(2)}, u32[]{:S(2)}) %all-to-all-start) | async-done | bytes 524320 | tf_op jit(solution)/shard_map/all_to_all | solution.py:578
  39.5 0.0 copy-start
  39.5 0.8 copy-done
  40.4 3.5 %focal.1 = bf16[8,2,128,128]{3,2,1,0:T(8,128)(2,1)} custom-call(bf16[8,2,128,128]{3,2,1,0:T(8,128)(2,1)} %copy-done, f32[2,128,512]{2,1,0:T(8,128)} %reshape.10.target_ref, bf16[2,1024,512]{2,1,0:T(8,128)(2,1)} %row_table.1.table_ref), custom_call_target="tpu_custom_call" | custom-call | flops 536870912 | bytes 4000000 | tf_op jit(solution)/shard_map/focal/pallas_call | solution.py:598
  43.9 19.5 %all_to_all.15.h_ref = bf16[8,2,128,128]{3,2,1,0:T(8,128)(2,1)} all-to-all(bf16[8,2,128,128]{3,2,1,0:T(8,128)(2,1)} %focal.1), channel_id=1, replica_groups=mesh['band'=4,'row'=8] {'row'}, dimensions={0} | all-to-all | bytes 1048576 | tf_op jit(solution)/shard_map/all_to_all | solution.py:612
  63.3 11.1 %weight.1 = (f32[15,128]{1,0:T(8,128)}, f32[15,128]{1,0:T(8,128)}) custom-call(s32[2]{0:T(128)} %pad_add_fusion.pos_ref, s32[4,1200]{1,0:T(4,128)} %box_ref.3, bf16[8,2,128,128]{3,2,1,0:T(8,128)(2,1)} %all_to_all.15.h_ref, bf16[2,2,256,4096]{3,2,1,0:T(8,128)(2,1)} %get-tuple-element.14.x_ref, f32[2,128,256]{2,1,0:T(8,128)} %get-tuple-element.15.tile_ref, ...), custom_call_target="tpu_custom_call" | custom-call | flops 4294967296 | bytes 20000000 | tf_op jit(solution)/shard_map/weight/pallas_call | solution.py:628
  74.4 0.4 collective-permute-start
  74.8 1.0 %collective-permute-done = f32[15,128]{1,0:T(8,128)S(1)} collective-permute-done((f32[15,128]{1,0:T(8,128)}, f32[15,128]{1,0:T(8,128)S(1)}, u32[]{:S(2)}, u32[]{:S(2)}) %collective-permute-start) | collective-permute-done | bytes 7712 | tf_op jit(solution)/shard_map/ppermute | solution.py:660
  75.9 0.7 add.12
  76.6 14.3 %all_to_all.16 = f32[16,15,128]{2,1,0:T(8,128)S(1)} all-to-all(f32[16,15,128]{2,1,0:T(8,128)S(1)} %broadcast_in_dim.2), channel_id=1, replica_groups={{0,2,4,6,8,10,12,14,16,18,20,22,24,26,28,30},{1,3,5,7,9,11,13,15,17,19,..., dimensions={0} | all-to-all | bytes 245760 | tf_op jit(solution)/shard_map/all_to_all | solution.py:664
  90.9 0.1 collective-permute-start.1
  91.0 1.1 %collective-permute-done.1 = f32[15,128]{1,0:T(8,128)S(1)} collective-permute-done((f32[15,128]{1,0:T(8,128)S(1)}, f32[15,128]{1,0:T(8,128)S(1)}, u32[]{:S(2)}, u32[]{:S(2)}) %collective-permute-start.1) | collective-permute-done | bytes 7712 | tf_op jit(solution)/shard_map/ppermute | solution.py:660
  92.2 0.6 pad_maximum_fusion
  (5 shorter events, 0.1 us)
Async XLA Ops:
  0.6 23.6 %copy-start.1 = (f32[2,32,4,2,256]{4,3,2,1,0:T(2,128)S(1)}, f32[2,32,4,2,256]{4,3,2,1,0:T(2,128)}, u32[]{:S(2)}) copy-start(f32[2,32,4,2,256]{4,3,2,1,0:T(2,128)} %param.13) | copy-start | bytes 1572868
  17.8 21.7 %all-to-all-start = ((bf16[8,2,128,128]{3,2,1,0:T(8,128)(2,1)}), bf16[8,2,128,128]{3,2,1,0:T(8,128)(2,1)S(1)}, u32[]{:S(2)}, u32[]{:S(2)}) async-start(bf16[8,2,128,128]{3,2,1,0:T(8,128)(2,1)} %get-tuple-element.13), calls=%async_computation | async-start | bytes 1048576 | tf_op jit(solution)/shard_map/all_to_all | solution.py:578
  39.5 0.8 copy-start
  74.4 1.4 %collective-permute-start = (f32[15,128]{1,0:T(8,128)}, f32[15,128]{1,0:T(8,128)S(1)}, u32[]{:S(2)}, u32[]{:S(2)}) collective-permute-start(f32[15,128]{1,0:T(8,128)} %get-tuple-element.20), channel_id=1, source_target_pairs={{0,1},{1,0},{2,3},{3,2},{4,5},{5,4},{6,7},{7,6},{8,9},{9,8},{10,11... | collective-permute-start | bytes 23048 | tf_op jit(solution)/shard_map/ppermute | solution.py:660
  90.9 1.2 %collective-permute-start.1 = (f32[15,128]{1,0:T(8,128)S(1)}, f32[15,128]{1,0:T(8,128)S(1)}, u32[]{:S(2)}, u32[]{:S(2)}) collective-permute-start(f32[15,128]{1,0:T(8,128)S(1)} %reduce_sum.9), channel_id=1, source_target_pairs={{0,1},{1,0},{2,3},{3,2},{4,5},{5,4},{6,7},{7,6},{8,9},{9,8},{10,11... | collective-permute-start | bytes 23048 | tf_op jit(solution)/shard_map/ppermute | solution.py:660

commit v4 on v3

--- a/solution.py
+++ b/solution.py
@@ -14,7 +14,7 @@
 TWO_PI = 2.0 * math.pi
 LANES = 128
 F32 = jnp.float32
-BLOCKS = (512, 2048, 512)
+BLOCKS = (512, 2048, 256)
 BF16 = jnp.bfloat16
 
 SIN_HALF = (0.9999999971, -0.1666666029, 0.008333109246, -0.0001981365728, 2.616271295e-06)
@@ -359,7 +359,7 @@
 def weight_kernel(
     dims, pos_ref, box_ref, h_ref, x_ref, tile_ref, shift_ref, across_ref, index_ref,
     out_ref, give_ref, left_ref, pick_ref, cos_ref, sin_ref, p_ref, q_ref, weight_ref, sums_ref,
-    term_ref, flat_ref,
+    term_ref, flat_ref, slot_ref,
 ):
     rows, cols, block, part, bands, half, per_row, pairs, vloc, sources, scale = dims
     step = pl.program_id(0)
@@ -451,16 +451,19 @@
                     )
                 return total
 
-            total = lax.fori_loop(0, pl.num_programs(0), add, jnp.zeros((8, LANES), F32))
-            total = jnp.where(iota((8, LANES), 1) < per_row, total, 0.0)
+            total = lax.fori_loop(0, pl.num_programs(0), add, jnp.zeros((8, padded), F32))
+            slot_ref[:, :padded] = total
+            total = jnp.where(iota((8, LANES), 1) < per_row, slot_ref[...], 0.0)
             padding = jnp.zeros((8, flat_ref.shape[1] - LANES), F32)
             wide = jnp.concatenate([total, padding], axis=1)
             flat_ref[...] += pltpu.roll(wide, t * per_row, axis=1)
             return carry
 
-        tile_index = iota((LANES, block), 0).astype(F32).astype(BF16)
-        one = jnp.ones((LANES, block), BF16)
-        zero = jnp.zeros((LANES, block), BF16)
+        padded = -(-per_row // 16) * 16
+        tile_index = iota((padded, block), 0).astype(F32).astype(BF16)
+        one = jnp.ones((padded, block), BF16)
+        zero = jnp.zeros((padded, block), BF16)
+        slot_ref[...] = jnp.zeros_like(slot_ref)
         flat_ref[...] = jnp.zeros_like(flat_ref)
         lax.fori_loop(first, last, tile_row, 0)
         odd = pos_ref[0] % 2 == 1
@@ -646,6 +649,7 @@
             pltpu.VMEM((steps, 2, 3, SROWS, block), F32),
             pltpu.VMEM((steps, 2, SROWS, block), jnp.int32),
             pltpu.VMEM((8, 2 * pieces * LANES), F32),
+            pltpu.VMEM((8, LANES), F32),
         ],
         compiler_params=params,
         cost_estimate=cost(4 * matmul, 20e6),

time: 92.7 us -> 91.8 us (level)
  blocking collectives: 33.8 us -> 32 us
    all_to_all x1, blocking collectives: 14.3 us -> 12.6 us  [body(): lax.all_to_all(copies, axes, split_axis=0, concat_axis=0, tiled=True, axi...]
where the time goes in v4:
time: 91.8 us; the launch traced here: 91 us
  Pallas kernels  34.5 us (38%)
  blocking collectives  32 us (35%)
  waiting for transfers between devices  13 us (14%)
  starting transfers between devices  6.44 us (7%)
  other arithmetic  2.8 us (3%)
  local copies, waits for them, and re-layouts  2.26 us (2%)
    all_to_all x1, blocking collectives, body(): lax.all_to_all(spread, 'row', split_axis=0, concat_axis=0, tiled=True)  19.5 us
    pallas_call x1, Pallas kernels, body(): pl.pallas_call(functools.partial(field_kernel, (field_dims(field_block),...  17.2 us
    all_to_all x1, blocking collectives, body(): lax.all_to_all(copies, axes, split_axis=0, concat_axis=0, tiled=True, axi...  12.6 us
    pallas_call x1, Pallas kernels, body(): pl.pallas_call(functools.partial(weight_kernel, weight_dims), grid=(steps...  11.1 us
    all_to_all x1, waiting for transfers between devices, body(): lax.all_to_all(half_way, 'row', split_axis=0, concat_axis=0, tiled=True)  10.4 us
    all_to_all x1, starting transfers between devices, body(): lax.all_to_all(half_way, 'row', split_axis=0, concat_axis=0, tiled=True)  6.37 us
    pallas_call x1, Pallas kernels, body(): pl.pallas_call(functools.partial(focal_kernel, (rows, owners, normf)), gr...  3.53 us
    pallas_call x1, Pallas kernels, body(): pl.pallas_call(functools.partial(row_table_kernel, (rows, cols, bands, fo...  2.58 us
  transfers between devices with their start and end apart: 3, of which 3 were waited for; matrix products, arithmetic and copies ran while one was open for 2% of the time, Pallas kernels for 3%

profile of v4, /device:TPU:0, one launch (start us, length us, event | category | flops | bytes accessed | tf_op | source)
XLA Modules:
  0.0 91.0 jit_solution(9856255465405719751)
XLA Ops:
  0.0 0.6 pad_add_fusion.pos_ref
  0.6 0.0 copy-start.1
  0.6 17.2 %field.1 = (bf16[2,2,256,4096]{3,2,1,0:T(8,128)(2,1)}, f32[2,128,256]{2,1,0:T(8,128)}, f32[2,32,256]{2,1,0:T(8,128)}, f32[2,16,4096]{2,1,0:T(8,128)}, s32[2,16,4...) custom-call(s32[2]{0:T(128)} %pad_add_fusion.pos_ref, s32[4,1200]{1,0:T(4,128)} %box_ref.3, s32[2,2]{1,0:T(2,128)} %freq_ref.1, ...), custom_call_target="tpu_custom_call" | custom-call | flops 4294967296 | bytes 20000000 | tf_op jit(solution)/shard_map/field/pallas_call | solution.py:532
  17.8 6.4 %all-to-all-start = ((bf16[8,2,128,128]{3,2,1,0:T(8,128)(2,1)}), bf16[8,2,128,128]{3,2,1,0:T(8,128)(2,1)S(1)}, u32[]{:S(2)}, u32[]{:S(2)}) async-start(bf16[8,2,128,128]{3,2,1,0:T(8,128)(2,1)} %get-tuple-element.13), calls=%async_computation | async-start | bytes 1048576 | tf_op jit(solution)/shard_map/all_to_all | solution.py:581
  24.2 0.0 copy-done.1
  24.2 0.2 add_bitcast_fusion
  24.4 0.2 fusion
  24.6 0.2 maximum_bitcast_fusion.1
  24.9 0.2 maximum_bitcast_fusion
  25.1 0.2 copy.10
  25.3 1.2 %reshape.10.target_ref = f32[2,128,512]{2,1,0:T(8,128)} reshape(f32[2,2,2,32,2,256]{5,4,3,2,1,0:T(2,128)S(1)} %copy.10) | data formatting | bytes 1048576 | tf_op jit(solution)/shard_map/reshape | solution.py:598
  26.5 2.6 %row_table.1.table_ref = bf16[2,1024,512]{2,1,0:T(8,128)(2,1)} custom-call(s32[2]{0:T(128)} %pad_add_fusion.pos_ref), custom_call_target="tpu_custom_call" | custom-call | flops 1000000 | bytes 2000000 | tf_op jit(solution)/shard_map/row_table/pallas_call | solution.py:583
  29.1 10.4 %all-to-all-done.y_ref = bf16[8,2,128,128]{3,2,1,0:T(8,128)(2,1)S(1)} async-done(((bf16[8,2,128,128]{3,2,1,0:T(8,128)(2,1)}), bf16[8,2,128,128]{3,2,1,0:T(8,128)(2,1)S(1)}, u32[]{:S(2)}, u32[]{:S(2)}) %all-to-all-start) | async-done | bytes 524320 | tf_op jit(solution)/shard_map/all_to_all | solution.py:581
  39.5 0.0 copy-start
  39.5 0.8 copy-done
  40.4 3.5 %focal.1 = bf16[8,2,128,128]{3,2,1,0:T(8,128)(2,1)} custom-call(bf16[8,2,128,128]{3,2,1,0:T(8,128)(2,1)} %copy-done, f32[2,128,512]{2,1,0:T(8,128)} %reshape.10.target_ref, bf16[2,1024,512]{2,1,0:T(8,128)(2,1)} %row_table.1.table_ref), custom_call_target="tpu_custom_call" | custom-call | flops 536870912 | bytes 4000000 | tf_op jit(solution)/shard_map/focal/pallas_call | solution.py:601
  43.9 19.5 %all_to_all.15.h_ref = bf16[8,2,128,128]{3,2,1,0:T(8,128)(2,1)} all-to-all(bf16[8,2,128,128]{3,2,1,0:T(8,128)(2,1)} %focal.1), channel_id=1, replica_groups=mesh['band'=4,'row'=8] {'row'}, dimensions={0} | all-to-all | bytes 1048576 | tf_op jit(solution)/shard_map/all_to_all | solution.py:615
  63.3 11.1 %weight.1 = (f32[15,128]{1,0:T(8,128)}, f32[15,128]{1,0:T(8,128)}) custom-call(s32[2]{0:T(128)} %pad_add_fusion.pos_ref, s32[4,1200]{1,0:T(4,128)} %box_ref.3, bf16[8,2,128,128]{3,2,1,0:T(8,128)(2,1)} %all_to_all.15.h_ref, bf16[2,2,256,4096]{3,2,1,0:T(8,128)(2,1)} %get-tuple-element.14.x_ref, f32[2,128,256]{2,1,0:T(8,128)} %get-tuple-element.15.tile_ref, ...), custom_call_target="tpu_custom_call" | custom-call | flops 4294967296 | bytes 20000000 | tf_op jit(solution)/shard_map/weight/pallas_call | solution.py:631
  74.5 0.0 collective-permute-start
  74.5 1.4 %collective-permute-done = f32[15,128]{1,0:T(8,128)S(1)} collective-permute-done((f32[15,128]{1,0:T(8,128)}, f32[15,128]{1,0:T(8,128)S(1)}, u32[]{:S(2)}, u32[]{:S(2)}) %collective-permute-start) | collective-permute-done | bytes 7712 | tf_op jit(solution)/shard_map/ppermute | solution.py:664
  75.8 0.7 add.12
  76.6 12.6 %all_to_all.16 = f32[16,15,128]{2,1,0:T(8,128)S(1)} all-to-all(f32[16,15,128]{2,1,0:T(8,128)S(1)} %broadcast_in_dim.2), channel_id=1, replica_groups={{0,2,4,6,8,10,12,14,16,18,20,22,24,26,28,30},{1,3,5,7,9,11,13,15,17,19,..., dimensions={0} | all-to-all | bytes 245760 | tf_op jit(solution)/shard_map/all_to_all | solution.py:668
  89.1 0.1 collective-permute-start.1
  89.2 1.1 %collective-permute-done.1 = f32[15,128]{1,0:T(8,128)S(1)} collective-permute-done((f32[15,128]{1,0:T(8,128)S(1)}, f32[15,128]{1,0:T(8,128)S(1)}, u32[]{:S(2)}, u32[]{:S(2)}) %collective-permute-start.1) | collective-permute-done | bytes 7712 | tf_op jit(solution)/shard_map/ppermute | solution.py:664
  90.4 0.6 pad_maximum_fusion
  (5 shorter events, 0.1 us)
Async XLA Ops:
  0.6 23.6 %copy-start.1 = (f32[2,32,4,2,256]{4,3,2,1,0:T(2,128)S(1)}, f32[2,32,4,2,256]{4,3,2,1,0:T(2,128)}, u32[]{:S(2)}) copy-start(f32[2,32,4,2,256]{4,3,2,1,0:T(2,128)} %param.13) | copy-start | bytes 1572868
  17.8 21.7 %all-to-all-start = ((bf16[8,2,128,128]{3,2,1,0:T(8,128)(2,1)}), bf16[8,2,128,128]{3,2,1,0:T(8,128)(2,1)S(1)}, u32[]{:S(2)}, u32[]{:S(2)}) async-start(bf16[8,2,128,128]{3,2,1,0:T(8,128)(2,1)} %get-tuple-element.13), calls=%async_computation | async-start | bytes 1048576 | tf_op jit(solution)/shard_map/all_to_all | solution.py:581
  39.5 0.8 copy-start
  74.5 1.4 %collective-permute-start = (f32[15,128]{1,0:T(8,128)}, f32[15,128]{1,0:T(8,128)S(1)}, u32[]{:S(2)}, u32[]{:S(2)}) collective-permute-start(f32[15,128]{1,0:T(8,128)} %get-tuple-element.20), channel_id=1, source_target_pairs={{0,1},{1,0},{2,3},{3,2},{4,5},{5,4},{6,7},{7,6},{8,9},{9,8},{10,11... | collective-permute-start | bytes 23048 | tf_op jit(solution)/shard_map/ppermute | solution.py:664
  89.1 1.2 %collective-permute-start.1 = (f32[15,128]{1,0:T(8,128)S(1)}, f32[15,128]{1,0:T(8,128)S(1)}, u32[]{:S(2)}, u32[]{:S(2)}) collective-permute-start(f32[15,128]{1,0:T(8,128)S(1)} %reduce_sum.9), channel_id=1, source_target_pairs={{0,1},{1,0},{2,3},{3,2},{4,5},{5,4},{6,7},{7,6},{8,9},{9,8},{10,11... | collective-permute-start | bytes 23048 | tf_op jit(solution)/shard_map/ppermute | solution.py:664

commit v5 on v4

--- a/solution.py
+++ b/solution.py
@@ -608,7 +608,9 @@
         ],
         out_specs=y_block,
         out_shape=jax.ShapeDtypeStruct((owners, bands, arrays * vloc, r2), BF16),
-        compiler_params=params,
+        compiler_params=pltpu.CompilerParams(
+            dimension_semantics=("arbitrary",), vmem_limit_bytes=24 << 20
+        ),
         cost_estimate=cost(8 * bands * arrays * vloc * owners * r2 * focal, 4e6),
         name="focal",
     )(received, targets, row_table)

time: 91.8 us -> 89.1 us (0.971)
  Pallas kernels: 34.5 us -> 31.6 us
  starting transfers between devices: 6.44 us -> 7.39 us
    pallas_call x1, Pallas kernels: 3.53 us -> 1.47 us  [body(): pl.pallas_call(functools.partial(focal_kernel, (rows, owners, normf)), gr...]
    all_to_all x1, blocking collectives: 19.5 us -> 18.4 us  [body(): lax.all_to_all(spread, 'row', split_axis=0, concat_axis=0, tiled=True)]
    ppermute x2, starting transfers between devices: 0.07 us -> 1.04 us  [swap_cores(): return lax.ppermute(array, 'row', [(i, i ^ 1) for i in range(owners)])]
where the time goes in v5:
time: 89.1 us; the launch traced here: 88.7 us
  Pallas kernels  31.6 us (35%)
  blocking collectives  31.1 us (35%)
  waiting for transfers between devices  13.4 us (15%)
  starting transfers between devices  7.39 us (8%)
  other arithmetic  2.87 us (3%)
  local copies, waits for them, and re-layouts  2.23 us (3%)
    all_to_all x1, blocking collectives, body(): lax.all_to_all(spread, 'row', split_axis=0, concat_axis=0, tiled=True)  18.4 us
    pallas_call x1, Pallas kernels, body(): pl.pallas_call(functools.partial(field_kernel, (field_dims(field_block),...  17.2 us
    all_to_all x1, blocking collectives, body(): lax.all_to_all(copies, axes, split_axis=0, concat_axis=0, tiled=True, axi...  12.7 us
    all_to_all x1, waiting for transfers between devices, body(): lax.all_to_all(half_way, 'row', split_axis=0, concat_axis=0, tiled=True)  11.2 us
    pallas_call x1, Pallas kernels, body(): pl.pallas_call(functools.partial(weight_kernel, weight_dims), grid=(steps...  10.4 us
    all_to_all x1, starting transfers between devices, body(): lax.all_to_all(half_way, 'row', split_axis=0, concat_axis=0, tiled=True)  6.35 us
    pallas_call x1, Pallas kernels, body(): pl.pallas_call(functools.partial(row_table_kernel, (rows, cols, bands, fo...  2.58 us
    ppermute x2, waiting for transfers between devices, swap_cores(): return lax.ppermute(array, 'row', [(i, i ^ 1) for i in range(owners)])  2.19 us
  transfers between devices with their start and end apart: 3, of which 3 were waited for; matrix products, arithmetic and copies ran while one was open for 2% of the time, Pallas kernels for 3%

profile of v5, /device:TPU:0, one launch (start us, length us, event | category | flops | bytes accessed | tf_op | source)
XLA Modules:
  0.0 88.7 jit_solution(711215654516996935)
XLA Ops:
  0.0 0.7 pad_add_fusion.pos_ref
  0.7 0.0 copy-start.1
  0.7 17.2 %field.1 = (bf16[2,2,256,4096]{3,2,1,0:T(8,128)(2,1)}, f32[2,128,256]{2,1,0:T(8,128)}, f32[2,32,256]{2,1,0:T(8,128)}, f32[2,16,4096]{2,1,0:T(8,128)}, s32[2,16,4...) custom-call(s32[2]{0:T(128)} %pad_add_fusion.pos_ref, s32[4,1200]{1,0:T(4,128)} %box_ref.3, s32[2,2]{1,0:T(2,128)} %freq_ref.1, ...), custom_call_target="tpu_custom_call" | custom-call | flops 4294967296 | bytes 20000000 | tf_op jit(solution)/shard_map/field/pallas_call | solution.py:532
  17.9 6.4 %all-to-all-start = ((bf16[8,2,128,128]{3,2,1,0:T(8,128)(2,1)}), bf16[8,2,128,128]{3,2,1,0:T(8,128)(2,1)S(1)}, u32[]{:S(2)}, u32[]{:S(2)}) async-start(bf16[8,2,128,128]{3,2,1,0:T(8,128)(2,1)} %get-tuple-element.13), calls=%async_computation | async-start | bytes 1048576 | tf_op jit(solution)/shard_map/all_to_all | solution.py:581
  24.2 0.0 copy-done.1
  24.2 0.2 add_bitcast_fusion
  24.4 0.2 fusion
  24.6 0.2 maximum_bitcast_fusion.1
  24.9 0.2 maximum_bitcast_fusion
  25.1 0.2 copy.10
  25.3 0.4 reshape.10.target_ref
  25.8 2.6 %row_table.1.table_ref = bf16[2,1024,512]{2,1,0:T(8,128)(2,1)} custom-call(s32[2]{0:T(128)} %pad_add_fusion.pos_ref), custom_call_target="tpu_custom_call" | custom-call | flops 1000000 | bytes 2000000 | tf_op jit(solution)/shard_map/row_table/pallas_call | solution.py:583
  28.3 11.2 %all-to-all-done.y_ref = bf16[8,2,128,128]{3,2,1,0:T(8,128)(2,1)S(1)} async-done(((bf16[8,2,128,128]{3,2,1,0:T(8,128)(2,1)}), bf16[8,2,128,128]{3,2,1,0:T(8,128)(2,1)S(1)}, u32[]{:S(2)}, u32[]{:S(2)}) %all-to-all-start) | async-done | bytes 524320 | tf_op jit(solution)/shard_map/all_to_all | solution.py:581
  39.6 0.0 copy-start
  39.6 1.6 %copy-done = bf16[2,1024,512]{2,1,0:T(8,128)(2,1)S(1)} copy-done((bf16[2,1024,512]{2,1,0:T(8,128)(2,1)S(1)}, bf16[2,1024,512]{2,1,0:T(8,128)(2,1)}, u32[]{:S(2)}) %copy-start) | copy-done | bytes 2097176
  41.2 1.5 %focal.1 = bf16[8,2,128,128]{3,2,1,0:T(8,128)(2,1)S(1)} custom-call(bf16[8,2,128,128]{3,2,1,0:T(8,128)(2,1)S(1)} %all-to-all-done.y_ref, f32[2,128,512]{2,1,0:T(8,128)S(1)} %reshape.10.target_ref, bf16[2,1024,512]{2,1,0:T(8,128)(2,1)S(1)} %copy-done), custom_call_target="tpu_custom_call" | custom-call | flops 536870912 | bytes 4000000 | tf_op jit(solution)/shard_map/focal/pallas_call | solution.py:601
  42.6 18.4 %all_to_all.15.h_ref = bf16[8,2,128,128]{3,2,1,0:T(8,128)(2,1)} all-to-all(bf16[8,2,128,128]{3,2,1,0:T(8,128)(2,1)S(1)} %focal.1), channel_id=1, replica_groups=mesh['band'=4,'row'=8] {'row'}, dimensions={0} | all-to-all | bytes 1048576 | tf_op jit(solution)/shard_map/all_to_all | solution.py:617
  61.0 10.4 %weight.1 = (f32[15,128]{1,0:T(8,128)}, f32[15,128]{1,0:T(8,128)}) custom-call(s32[2]{0:T(128)} %pad_add_fusion.pos_ref, s32[4,1200]{1,0:T(4,128)} %box_ref.3, bf16[8,2,128,128]{3,2,1,0:T(8,128)(2,1)} %all_to_all.15.h_ref, bf16[2,2,256,4096]{3,2,1,0:T(8,128)(2,1)} %get-tuple-element.14.x_ref, f32[2,128,256]{2,1,0:T(8,128)} %get-tuple-element.15.tile_ref, ...), custom_call_target="tpu_custom_call" | custom-call | flops 4294967296 | bytes 20000000 | tf_op jit(solution)/shard_map/weight/pallas_call | solution.py:633
  71.4 1.0 %collective-permute-start = (f32[15,128]{1,0:T(8,128)}, f32[15,128]{1,0:T(8,128)S(1)}, u32[]{:S(2)}, u32[]{:S(2)}) collective-permute-start(f32[15,128]{1,0:T(8,128)} %get-tuple-element.20), channel_id=1, source_target_pairs={{0,1},{1,0},{2,3},{3,2},{4,5},{5,4},{6,7},{7,6},{8,9},{9,8},{10,11... | collective-permute-start | bytes 23048 | tf_op jit(solution)/shard_map/ppermute | solution.py:666
  72.4 1.0 %collective-permute-done = f32[15,128]{1,0:T(8,128)S(1)} collective-permute-done((f32[15,128]{1,0:T(8,128)}, f32[15,128]{1,0:T(8,128)S(1)}, u32[]{:S(2)}, u32[]{:S(2)}) %collective-permute-start) | collective-permute-done | bytes 7712 | tf_op jit(solution)/shard_map/ppermute | solution.py:666
  73.4 0.7 add.12
  74.1 12.7 %all_to_all.16 = f32[16,15,128]{2,1,0:T(8,128)S(1)} all-to-all(f32[16,15,128]{2,1,0:T(8,128)S(1)} %broadcast_in_dim.2), channel_id=1, replica_groups={{0,2,4,6,8,10,12,14,16,18,20,22,24,26,28,30},{1,3,5,7,9,11,13,15,17,19,..., dimensions={0} | all-to-all | bytes 245760 | tf_op jit(solution)/shard_map/all_to_all | solution.py:670
  86.8 0.1 collective-permute-start.1
  86.9 1.1 %collective-permute-done.1 = f32[15,128]{1,0:T(8,128)S(1)} collective-permute-done((f32[15,128]{1,0:T(8,128)S(1)}, f32[15,128]{1,0:T(8,128)S(1)}, u32[]{:S(2)}, u32[]{:S(2)}) %collective-permute-start.1) | collective-permute-done | bytes 7712 | tf_op jit(solution)/shard_map/ppermute | solution.py:666
  88.1 0.6 pad_maximum_fusion
  (5 shorter events, 0.1 us)
Async XLA Ops:
  0.7 23.6 %copy-start.1 = (f32[2,32,4,2,256]{4,3,2,1,0:T(2,128)S(1)}, f32[2,32,4,2,256]{4,3,2,1,0:T(2,128)}, u32[]{:S(2)}) copy-start(f32[2,32,4,2,256]{4,3,2,1,0:T(2,128)} %param.13) | copy-start | bytes 1572868
  17.9 21.7 %all-to-all-start = ((bf16[8,2,128,128]{3,2,1,0:T(8,128)(2,1)}), bf16[8,2,128,128]{3,2,1,0:T(8,128)(2,1)S(1)}, u32[]{:S(2)}, u32[]{:S(2)}) async-start(bf16[8,2,128,128]{3,2,1,0:T(8,128)(2,1)} %get-tuple-element.13), calls=%async_computation | async-start | bytes 1048576 | tf_op jit(solution)/shard_map/all_to_all | solution.py:581
  39.6 1.6 %copy-start = (bf16[2,1024,512]{2,1,0:T(8,128)(2,1)S(1)}, bf16[2,1024,512]{2,1,0:T(8,128)(2,1)}, u32[]{:S(2)}) copy-start(bf16[2,1024,512]{2,1,0:T(8,128)(2,1)} %row_table.1.table_ref) | copy-start | bytes 6291460
  71.4 2.0 %collective-permute-start = (f32[15,128]{1,0:T(8,128)}, f32[15,128]{1,0:T(8,128)S(1)}, u32[]{:S(2)}, u32[]{:S(2)}) collective-permute-start(f32[15,128]{1,0:T(8,128)} %get-tuple-element.20), channel_id=1, source_target_pairs={{0,1},{1,0},{2,3},{3,2},{4,5},{5,4},{6,7},{7,6},{8,9},{9,8},{10,11... | collective-permute-start | bytes 23048 | tf_op jit(solution)/shard_map/ppermute | solution.py:666
  86.8 1.2 %collective-permute-start.1 = (f32[15,128]{1,0:T(8,128)S(1)}, f32[15,128]{1,0:T(8,128)S(1)}, u32[]{:S(2)}, u32[]{:S(2)}) collective-permute-start(f32[15,128]{1,0:T(8,128)S(1)} %reduce_sum.9), channel_id=1, source_target_pairs={{0,1},{1,0},{2,3},{3,2},{4,5},{5,4},{6,7},{7,6},{8,9},{9,8},{10,11... | collective-permute-start | bytes 23048 | tf_op jit(solution)/shard_map/ppermute | solution.py:666

commit v6 on v5

--- a/solution.py
+++ b/solution.py
@@ -653,7 +653,9 @@
             pltpu.VMEM((8, 2 * pieces * LANES), F32),
             pltpu.VMEM((8, LANES), F32),
         ],
-        compiler_params=params,
+        compiler_params=pltpu.CompilerParams(
+            dimension_semantics=("arbitrary",), vmem_limit_bytes=51 << 20
+        ),
         cost_estimate=cost(4 * matmul, 20e6),
         name="weight",
     )(pos, seg_box, hidden, fields, tile, shift, across, index)

time: 89.1 us -> 87 us (0.976)
  Pallas kernels: 31.6 us -> 30.7 us
    all_to_all x1, blocking collectives: 12.7 us -> 14.1 us  [body(): lax.all_to_all(copies, axes, split_axis=0, concat_axis=0, tiled=True, axi...]
    pallas_call x1, Pallas kernels: 10.4 us -> 9.36 us  [body(): pl.pallas_call(functools.partial(weight_kernel, weight_dims), grid=(steps...]
where the time goes in v6:
time: 87 us
  blocking collectives  31.8 us (37%)
  Pallas kernels  30.7 us (35%)
  waiting for transfers between devices  13.3 us (15%)
  starting transfers between devices  6.71 us (8%)
  local copies, waits for them, and re-layouts  2.26 us (3%)
  other arithmetic  2.13 us (2%)
    all_to_all x1, blocking collectives, body(): lax.all_to_all(spread, 'row', split_axis=0, concat_axis=0, tiled=True)  17.7 us
    pallas_call x1, Pallas kernels, body(): pl.pallas_call(functools.partial(field_kernel, (field_dims(field_block),...  17.2 us
    all_to_all x1, blocking collectives, body(): lax.all_to_all(copies, axes, split_axis=0, concat_axis=0, tiled=True, axi...  14.1 us
    all_to_all x1, waiting for transfers between devices, body(): lax.all_to_all(half_way, 'row', split_axis=0, concat_axis=0, tiled=True)  11.2 us
    pallas_call x1, Pallas kernels, body(): pl.pallas_call(functools.partial(weight_kernel, weight_dims), grid=(steps...  9.36 us
    all_to_all x1, starting transfers between devices, body(): lax.all_to_all(half_way, 'row', split_axis=0, concat_axis=0, tiled=True)  6.35 us
    pallas_call x1, Pallas kernels, body(): pl.pallas_call(functools.partial(row_table_kernel, (rows, cols, bands, fo...  2.59 us
    ppermute x2, waiting for transfers between devices, swap_cores(): return lax.ppermute(array, 'row', [(i, i ^ 1) for i in range(owners)])  2.09 us
  transfers between devices with their start and end apart: 3, of which 3 were waited for; matrix products, arithmetic and copies ran while one was open for 2% of the time, Pallas kernels for 3%

profile of v6, /device:TPU:0, one launch (start us, length us, event | category | flops | bytes accessed | tf_op | source)
XLA Modules:
  0.0 87.0 jit_solution(6457142920608279673)
XLA Ops:
  0.0 0.6 pad_add_fusion.pos_ref
  0.6 0.0 copy-start.7
  0.6 17.2 %field.1 = (bf16[2,2,256,4096]{3,2,1,0:T(8,128)(2,1)}, f32[2,128,256]{2,1,0:T(8,128)}, f32[2,32,256]{2,1,0:T(8,128)}, f32[2,16,4096]{2,1,0:T(8,128)}, s32[2,16,4...) custom-call(s32[2]{0:T(128)} %pad_add_fusion.pos_ref, s32[4,1200]{1,0:T(4,128)} %box_ref.3, s32[2,2]{1,0:T(2,128)} %freq_ref.1, ...), custom_call_target="tpu_custom_call" | custom-call | flops 4294967296 | bytes 20000000 | tf_op jit(solution)/shard_map/field/pallas_call | solution.py:532
  17.8 6.4 %all-to-all-start = ((bf16[8,2,128,128]{3,2,1,0:T(8,128)(2,1)}), bf16[8,2,128,128]{3,2,1,0:T(8,128)(2,1)S(1)}, u32[]{:S(2)}, u32[]{:S(2)}) async-start(bf16[8,2,128,128]{3,2,1,0:T(8,128)(2,1)} %get-tuple-element.13), calls=%async_computation | async-start | bytes 1048576 | tf_op jit(solution)/shard_map/all_to_all | solution.py:581
  24.2 0.0 copy-done.7
  24.2 0.2 add_bitcast_fusion
  24.4 0.2 fusion
  24.6 0.2 maximum_bitcast_fusion.1
  24.8 0.2 maximum_bitcast_fusion
  25.1 0.2 copy.10
  25.3 0.4 reshape.10.target_ref
  25.7 2.6 %row_table.1.table_ref = bf16[2,1024,512]{2,1,0:T(8,128)(2,1)} custom-call(s32[2]{0:T(128)} %pad_add_fusion.pos_ref), custom_call_target="tpu_custom_call" | custom-call | flops 1000000 | bytes 2000000 | tf_op jit(solution)/shard_map/row_table/pallas_call | solution.py:583
  28.3 11.2 %all-to-all-done.y_ref = bf16[8,2,128,128]{3,2,1,0:T(8,128)(2,1)S(1)} async-done(((bf16[8,2,128,128]{3,2,1,0:T(8,128)(2,1)}), bf16[8,2,128,128]{3,2,1,0:T(8,128)(2,1)S(1)}, u32[]{:S(2)}, u32[]{:S(2)}) %all-to-all-start) | async-done | bytes 524320 | tf_op jit(solution)/shard_map/all_to_all | solution.py:581
  39.5 0.0 copy-start
  39.5 1.6 %copy-done = bf16[2,1024,512]{2,1,0:T(8,128)(2,1)S(1)} copy-done((bf16[2,1024,512]{2,1,0:T(8,128)(2,1)S(1)}, bf16[2,1024,512]{2,1,0:T(8,128)(2,1)}, u32[]{:S(2)}) %copy-start) | copy-done | bytes 2097176
  41.1 0.0 copy-start.1
  41.1 0.0 copy-start.2
  41.1 0.0 copy-start.3
  41.1 0.0 copy-start.4
  41.1 0.0 copy-start.5
  41.1 0.0 copy-start.6
  41.1 1.5 %focal.1 = bf16[8,2,128,128]{3,2,1,0:T(8,128)(2,1)S(1)} custom-call(bf16[8,2,128,128]{3,2,1,0:T(8,128)(2,1)S(1)} %all-to-all-done.y_ref, f32[2,128,512]{2,1,0:T(8,128)S(1)} %reshape.10.target_ref, bf16[2,1024,512]{2,1,0:T(8,128)(2,1)S(1)} %copy-done), custom_call_target="tpu_custom_call" | custom-call | flops 536870912 | bytes 4000000 | tf_op jit(solution)/shard_map/focal/pallas_call | solution.py:601
  42.6 17.7 %all_to_all.15.h_ref = bf16[8,2,128,128]{3,2,1,0:T(8,128)(2,1)S(1)} all-to-all(bf16[8,2,128,128]{3,2,1,0:T(8,128)(2,1)S(1)} %focal.1), channel_id=1, replica_groups=mesh['band'=4,'row'=8] {'row'}, dimensions={0} | all-to-all | bytes 1048576 | tf_op jit(solution)/shard_map/all_to_all | solution.py:617
  60.4 0.0 copy-done.1
  60.4 0.0 copy-done.2
  60.4 0.0 copy-done.3
  60.4 0.0 copy-done.4
  60.4 0.0 copy-done.5
  60.4 0.0 copy-done.6
  60.4 9.4 %weight.1 = (f32[15,128]{1,0:T(8,128)S(1)}, f32[15,128]{1,0:T(8,128)S(1)}) custom-call(s32[2]{0:T(128)S(1)} %copy-done.1, s32[4,1200]{1,0:T(4,128)S(1)} %copy-done.2, bf16[8,2,128,128]{3,2,1,0:T(8,128)(2,1)S(1)} %all_to_all.15.h_ref, bf16[2,2,256,4096]{3,2,1,0:T(8,128)(2,1)} %get-tuple-element.14.x_ref, f32[2,128,256]{2,1,0:T(8,128)S(1)} %copy-done.5, ...), custom_call_target="tpu_custom_call" | custom-call | flops 4294967296 | bytes 20000000 | tf_op jit(solution)/shard_map/weight/pallas_call | solution.py:633
  69.8 0.3 collective-permute-start
  70.1 0.9 %collective-permute-done = f32[15,128]{1,0:T(8,128)S(1)} collective-permute-done((f32[15,128]{1,0:T(8,128)S(1)}, f32[15,128]{1,0:T(8,128)S(1)}, u32[]{:S(2)}, u32[]{:S(2)}) %collective-permute-start) | collective-permute-done | bytes 7712 | tf_op jit(solution)/shard_map/ppermute | solution.py:668
  71.1 14.1 %all_to_all.16 = f32[16,15,128]{2,1,0:T(8,128)S(1)} all-to-all(f32[16,15,128]{2,1,0:T(8,128)S(1)} %broadcast_in_dim.2), channel_id=1, replica_groups={{0,2,4,6,8,10,12,14,16,18,20,22,24,26,28,30},{1,3,5,7,9,11,13,15,17,19,..., dimensions={0} | all-to-all | bytes 245760 | tf_op jit(solution)/shard_map/all_to_all | solution.py:672
  85.1 0.1 collective-permute-start.1
  85.2 1.1 %collective-permute-done.1 = f32[15,128]{1,0:T(8,128)S(1)} collective-permute-done((f32[15,128]{1,0:T(8,128)S(1)}, f32[15,128]{1,0:T(8,128)S(1)}, u32[]{:S(2)}, u32[]{:S(2)}) %collective-permute-start.1) | collective-permute-done | bytes 7712 | tf_op jit(solution)/shard_map/ppermute | solution.py:668
  86.4 0.6 pad_maximum_fusion
  (6 shorter events, 0.1 us)
Async XLA Ops:
  0.6 23.6 %copy-start.7 = (f32[2,32,4,2,256]{4,3,2,1,0:T(2,128)S(1)}, f32[2,32,4,2,256]{4,3,2,1,0:T(2,128)}, u32[]{:S(2)}) copy-start(f32[2,32,4,2,256]{4,3,2,1,0:T(2,128)} %param.13) | copy-start | bytes 1572868
  17.8 21.7 %all-to-all-start = ((bf16[8,2,128,128]{3,2,1,0:T(8,128)(2,1)}), bf16[8,2,128,128]{3,2,1,0:T(8,128)(2,1)S(1)}, u32[]{:S(2)}, u32[]{:S(2)}) async-start(bf16[8,2,128,128]{3,2,1,0:T(8,128)(2,1)} %get-tuple-element.13), calls=%async_computation | async-start | bytes 1048576 | tf_op jit(solution)/shard_map/all_to_all | solution.py:581
  39.5 1.6 %copy-start = (bf16[2,1024,512]{2,1,0:T(8,128)(2,1)S(1)}, bf16[2,1024,512]{2,1,0:T(8,128)(2,1)}, u32[]{:S(2)}) copy-start(bf16[2,1024,512]{2,1,0:T(8,128)(2,1)} %row_table.1.table_ref) | copy-start | bytes 6291460
  41.1 19.3 %copy-start.1 = (s32[2]{0:T(128)S(1)}, s32[2]{0:T(128)}, u32[]{:S(2)}) copy-start(s32[2]{0:T(128)} %pad_add_fusion.pos_ref) | copy-start | bytes 28
  41.1 19.3 %copy-start.2 = (s32[4,1200]{1,0:T(4,128)S(1)}, s32[4,1200]{1,0:T(4,128)}, u32[]{:S(2)}) copy-start(s32[4,1200]{1,0:T(4,128)} %box_ref.3) | copy-start | bytes 57604
  41.1 19.3 %copy-start.3 = (f32[2,16,4096]{2,1,0:T(8,128)S(1)}, f32[2,16,4096]{2,1,0:T(8,128)}, u32[]{:S(2)}) copy-start(f32[2,16,4096]{2,1,0:T(8,128)} %get-tuple-element.17.across_ref) | copy-start | bytes 1572868
  41.1 19.3 %copy-start.4 = (s32[2,16,4096]{2,1,0:T(8,128)S(1)}, s32[2,16,4096]{2,1,0:T(8,128)}, u32[]{:S(2)}) copy-start(s32[2,16,4096]{2,1,0:T(8,128)} %get-tuple-element.18.index_ref) | copy-start | bytes 1572868
  41.1 19.3 %copy-start.5 = (f32[2,128,256]{2,1,0:T(8,128)S(1)}, f32[2,128,256]{2,1,0:T(8,128)}, u32[]{:S(2)}) copy-start(f32[2,128,256]{2,1,0:T(8,128)} %get-tuple-element.15.tile_ref) | copy-start | bytes 786436
  41.1 19.3 %copy-start.6 = (f32[2,32,256]{2,1,0:T(8,128)S(1)}, f32[2,32,256]{2,1,0:T(8,128)}, u32[]{:S(2)}) copy-start(f32[2,32,256]{2,1,0:T(8,128)} %get-tuple-element.16.shift_ref) | copy-start | bytes 196612
  69.8 1.2 %collective-permute-start = (f32[15,128]{1,0:T(8,128)S(1)}, f32[15,128]{1,0:T(8,128)S(1)}, u32[]{:S(2)}, u32[]{:S(2)}) collective-permute-start(f32[15,128]{1,0:T(8,128)S(1)} %get-tuple-element.20), channel_id=1, source_target_pairs={{0,1},{1,0},{2,3},{3,2},{4,5},{5,4},{6,7},{7,6},{8,9},{9,8},{10,11... | collective-permute-start | bytes 23048 | tf_op jit(solution)/shard_map/ppermute | solution.py:668
  85.1 1.2 %collective-permute-start.1 = (f32[15,128]{1,0:T(8,128)S(1)}, f32[15,128]{1,0:T(8,128)S(1)}, u32[]{:S(2)}, u32[]{:S(2)}) collective-permute-start(f32[15,128]{1,0:T(8,128)S(1)} %reduce_sum.9), channel_id=1, source_target_pairs={{0,1},{1,0},{2,3},{3,2},{4,5},{5,4},{6,7},{7,6},{8,9},{9,8},{10,11... | collective-permute-start | bytes 23048 | tf_op jit(solution)/shard_map/ppermute | solution.py:668
